TPU v7x, 32 devices: a whole 2x2x4 slice. The times are simulated.
32 devices in a mesh: gx: 4 (over z), gy: 2 (over x), gz: 4 (over y, core).
Axes of the slice: x: 2, y: 2, z: 4, core: 2. Of those that a mesh axis runs over, the one named last changes fastest.
Arguments:
- data: float32 [16, 512, 256], P('gz', 'gx', 'gy'), may hold values from -6 to 6
- weight: float32 [16, 512, 256], P('gz', 'gx', 'gy'), may hold values from 0.2 to 2
- dual_start: float32 [3, 16, 512, 256], P(None, 'gz', 'gx', 'gy'), may hold values from -3 to 3
- dual_mid: float32 [3, 16, 512, 256], P(None, 'gz', 'gx', 'gy'), may hold values from -3 to 3
- cotangent: float32 [3, 16, 512, 256], P(None, 'gz', 'gx', 'gy'), may hold values from -6 to 6
Outputs:
- dual_grad: float32 [3, 16, 512, 256], P(None, 'gz', 'gx', 'gy')
- weight_grad: float32 [16, 512, 256], P('gz', 'gx', 'gy')
- data_grad: float32 [16, 512, 256], P('gz', 'gx', 'gy')
All inputs are finite; a program needn't handle non-finite values.
Results may differ from a plain program's by a relative error of at most 0.00002.
Values sent between devices are 32-bit elements; how exact they have to be, the bound alone decides.
No kernel may reach another device: no remote copies, remote signals or barrier semaphores. Data moves between devices by JAX's collectives and lax.ppermute only.
A program may use at most 64 MiB of HBM per device.

v0:
```python
import jax
import jax.numpy as jnp
from jax import lax
from jax.sharding import PartitionSpec as P

step_size = 0.08
inverse_lambda = 0.5
smoothing = 0.01


def extended(cells, sides, width):
    for axis, dim in sides:
        count = lax.axis_size(axis)
        ends = count - 1
        head = lax.slice_in_dim(cells, 0, width, axis=dim)
        tail = lax.slice_in_dim(cells, cells.shape[dim] - width, cells.shape[dim], axis=dim)
        cells = jnp.concatenate(
            [
                lax.ppermute(tail, axis, [(i, (i + 1) % count) for i in range(ends)]),
                cells,
                lax.ppermute(head, axis, [((i + 1) % count, i) for i in range(ends)]),
            ],
            axis=dim,
        )
    return cells


def take(field, start, extent):
    return field[
        ...,
        start[0] : start[0] + extent[0],
        start[1] : start[1] + extent[1],
        start[2] : start[2] + extent[2],
    ]


def pad_cells(stack):
    return extended(stack, (("gx", 2), ("gy", 3), ("gz", 1)), 1)


def divergence(padded, extent):
    total = None
    for axis in range(3):
        lower = [1, 1, 1]
        lower[axis] = 0
        term = take(padded[axis], (1, 1, 1), extent) - take(padded[axis], tuple(lower), extent)
        total = term if total is None else total + term
    return total


def gradient(field, base, extent):
    center = take(field, (base, base, base), extent)
    parts = []
    for axis in range(3):
        upper = [base, base, base]
        upper[axis] = base + 1
        parts.append(take(field, tuple(upper), extent) - center)
    return jnp.stack(parts)


def edge_keep(count, is_last):
    places = jnp.arange(count + 1)
    return jnp.where(jnp.logical_and(is_last, places == count), 0.0, 1.0).astype(jnp.float32)


def local_adjoint(dual, slopes, weight, cot):
    norm = jnp.sqrt(jnp.sum(slopes * slopes, axis=0) + smoothing)
    denom = 1.0 + step_size * norm / weight
    update = (dual + step_size * slopes) / denom
    inner = jnp.sum(cot * update, axis=0)
    weight_part = inner * step_size * norm / (denom * weight * weight)
    norm_scale = -inner * step_size / (denom * weight)
    slope_cot = step_size * cot / denom + norm_scale / norm * slopes
    return (slope_cot, denom, weight_part)


def shards(data, weight, dual_start, dual_mid, cotangent):
    planes, rows, cols = data.shape
    inner_ext = (planes, rows, cols)
    outer_ext = (planes + 1, rows + 1, cols + 1)
    last_plane = lax.axis_index("gz") == lax.axis_size("gz") - 1
    last_row = lax.axis_index("gx") == lax.axis_size("gx") - 1
    last_col = lax.axis_index("gy") == lax.axis_size("gy") - 1
    keeper = (
        edge_keep(planes, last_plane)[:, None, None]
        * edge_keep(rows, last_row)[None, :, None]
        * edge_keep(cols, last_col)[None, None, :]
    )
    padded = pad_cells(jnp.concatenate([dual_start, dual_mid, data[None]], 0))
    scaled = take(padded[6], (1, 1, 1), outer_ext) * inverse_lambda
    slopes_start = gradient(keeper * (divergence(padded[0:3], outer_ext) - scaled), 0, inner_ext)
    slopes_mid = gradient(keeper * (divergence(padded[3:6], outer_ext) - scaled), 0, inner_ext)
    current = cotangent
    weight_parts = []
    data_parts = []
    for dual, slopes in ((dual_mid, slopes_mid), (dual_start, slopes_start)):
        slope_cot, denom, weight_part = local_adjoint(dual, slopes, weight, current)
        padded_cot = pad_cells(slope_cot)
        spread = keeper * -divergence(padded_cot, outer_ext)
        value_cot = spread[:planes, :rows, :cols]
        descent = gradient(spread, 0, inner_ext)
        current = current / denom - descent
        weight_parts.append(weight_part)
        data_parts.append(-value_cot * inverse_lambda)
    return (current, weight_parts[1] + weight_parts[0], data_parts[1] + data_parts[0])


def solution(mesh):
    in_specs = (
        P("gz", "gx", "gy"),
        P("gz", "gx", "gy"),
        P(None, "gz", "gx", "gy"),
        P(None, "gz", "gx", "gy"),
        P(None, "gz", "gx", "gy"),
    )
    out_specs = (P(None, "gz", "gx", "gy"), P("gz", "gx", "gy"), P("gz", "gx", "gy"))
    return jax.shard_map(shards, mesh=mesh, in_specs=in_specs, out_specs=out_specs, check_vma=False)
```

profile of v0, /device:TPU:1, one launch (start us, length us, event | category | flops | bytes accessed | tf_op | source)
XLA Modules:
  0.0 141.2 jit_solution(3618531319054938406)
XLA Ops:
  1.6 4.0 %collective-permute-start = (f32[7,4,1,128]{3,1,2,0:T(4,128)S(1)}, f32[7,4,1,128]{3,1,2,0:T(4,128)S(1)}, u32[]{:S(2)}, u32[]{:S(2)}) collective-permute-start(f32[7,4,1,128]{3,1,2,0:T(4,128)S(1)} %bitcast.83), channel_id=1, source_target_pairs={{0,8},{8,16},{16,24},{1,9},{9,17},{17,25},{2,10},{10,18},{18,26},{... | collective-permute-start | bytes 43016 | tf_op jit(solution)/shard_map/ppermute | solution.py:19
  6.9 3.3 %collective-permute-done.1 = f32[7,4,1,128]{3,1,2,0:T(4,128)} collective-permute-done((f32[7,4,1,128]{3,1,2,0:T(4,128)S(1)}, f32[7,4,1,128]{3,1,2,0:T(4,128)}, u32[]{:S(2)}, u32[]{:S(2)}) %collective-permute-start.1) | collective-permute-done | bytes 14368 | tf_op jit(solution)/shard_map/ppermute | solution.py:21
  11.8 1.9 %fusion.24 = (f32[7,4,130,1]{3,2,1,0:T(8,128)}, f32[7,4,130,1]{3,2,1,0:T(8,128)S(1)}) fusion(f32[7,4,130,128]{3,2,1,0:T(8,128)S(1)} %pad_maximum_fusion.3), kind=kLoop, calls=%fused_computation.115 | loop fusion | bytes 58240 | tf_op jit(solution)/shard_map/slice | solution.py:16
  13.7 3.2 %copy.67 = f32[7,4,130,1]{2,1,3,0:T(4,128)} copy(f32[7,4,130,1]{3,2,1,0:T(8,128)} %get-tuple-element.30) | data formatting | bytes 29120 | tf_op jit(solution)/shard_map/slice | solution.py:16
  16.9 3.7 %collective-permute-start.2 = (f32[7,4,130,1]{2,1,3,0:T(4,128)}, f32[7,4,130,1]{2,1,3,0:T(4,128)}, u32[]{:S(2)}, u32[]{:S(2)}) collective-permute-start(f32[7,4,130,1]{2,1,3,0:T(4,128)} %copy.67), channel_id=1, source_target_pairs={{0,4},{1,5},{2,6},{3,7},{8,12},{9,13},{10,14},{11,15},{16,20},{17,... | collective-permute-start | bytes 43688 | tf_op jit(solution)/shard_map/ppermute | solution.py:19
  20.7 1.7 %copy.68 = f32[7,4,130,1]{2,1,3,0:T(4,128)} copy(f32[7,4,130,1]{3,2,1,0:T(8,128)S(1)} %get-tuple-element.31) | data formatting | bytes 29120 | tf_op jit(solution)/shard_map/slice | solution.py:15
  25.0 2.2 %collective-permute-done.3 = f32[7,4,130,1]{2,1,3,0:T(4,128)} collective-permute-done((f32[7,4,130,1]{2,1,3,0:T(4,128)}, f32[7,4,130,1]{2,1,3,0:T(4,128)}, u32[]{:S(2)}, u32[]{:S(2)}) %collective-permute-start.3) | collective-permute-done | bytes 14592 | tf_op jit(solution)/shard_map/ppermute | solution.py:21
  27.2 2.7 %copy.70 = f32[7,4,130,1]{3,2,1,0:T(8,128)} copy(f32[7,4,130,1]{2,1,3,0:T(4,128)} %collective-permute-done.3) | data formatting | bytes 29120 | tf_op jit(solution)/shard_map/ppermute | solution.py:21
  30.0 2.1 %pad_maximum_fusion.10 = (f32[7,1,130,130]{3,2,1,0:T(8,128)S(1)}, f32[7,1,130,130]{3,2,1,0:T(8,128)S(1)}) fusion(f32[7,4,130,1]{3,2,1,0:T(8,128)} %copy.70, f32[7,4,130,1]{3,2,1,0:T(8,128)S(1)} %copy.69, f32[7,4,1,128]{3,2,1,0:T(1,128)} %bitcast.4, f32[7,4,1,128]{3,2,1,0:T(1,128)S(1)} %bitcast.68, f32[1,4,128,128]{3,2,1,0:T(8,128)} %bitcast.65, ...), kind=kLoop, calls=%fused_computation.14 | loop fusion | flops 1419600 | bytes 2839200 | tf_op jit(solution)/shard_map/slice | solution.py:16
  32.0 1.9 %copy.71 = f32[7,1,130,130]{3,1,2,0:T(1,128)} copy(f32[7,1,130,130]{3,2,1,0:T(8,128)S(1)} %get-tuple-element.18) | data formatting | bytes 946400 | tf_op jit(solution)/shard_map/slice | solution.py:16
  33.9 6.6 %collective-permute-start.4 = (f32[7,1,130,130]{3,1,2,0:T(1,128)}, f32[7,1,130,130]{3,1,2,0:T(1,128)}, u32[]{:S(2)}, u32[]{:S(2)}) collective-permute-start(f32[7,1,130,130]{3,1,2,0:T(1,128)} %copy.71), channel_id=1, source_target_pairs={{0,1},{1,2},{2,3},{4,5},{5,6},{6,7},{8,9},{9,10},{10,11},{12,13},{... | collective-permute-start | bytes 1419608 | tf_op jit(solution)/shard_map/ppermute | solution.py:19
  40.5 1.9 %copy.72 = f32[7,1,130,130]{3,1,2,0:T(1,128)} copy(f32[7,1,130,130]{3,2,1,0:T(8,128)S(1)} %get-tuple-element.19) | data formatting | bytes 946400 | tf_op jit(solution)/shard_map/slice | solution.py:15
  42.4 2.1 %collective-permute-start.5 = (f32[7,1,130,130]{3,1,2,0:T(1,128)}, f32[7,1,130,130]{3,1,2,0:T(1,128)}, u32[]{:S(2)}, u32[]{:S(2)}) collective-permute-start(f32[7,1,130,130]{3,1,2,0:T(1,128)} %copy.72), channel_id=1, source_target_pairs={{1,0},{2,1},{3,2},{5,4},{6,5},{7,6},{9,8},{10,9},{11,10},{13,12},{... | collective-permute-start | bytes 1419608 | tf_op jit(solution)/shard_map/ppermute | solution.py:21
  44.6 6.6 %collective-permute-done.4 = f32[7,1,130,130]{3,1,2,0:T(1,128)} collective-permute-done((f32[7,1,130,130]{3,1,2,0:T(1,128)}, f32[7,1,130,130]{3,1,2,0:T(1,128)}, u32[]{:S(2)}, u32[]{:S(2)}) %collective-permute-start.4) | collective-permute-done | bytes 473232 | tf_op jit(solution)/shard_map/ppermute | solution.py:19
  52.5 5.0 %collective-permute-done.5 = f32[7,1,130,130]{3,1,2,0:T(1,128)} collective-permute-done((f32[7,1,130,130]{3,1,2,0:T(1,128)}, f32[7,1,130,130]{3,1,2,0:T(1,128)}, u32[]{:S(2)}, u32[]{:S(2)}) %collective-permute-start.5) | collective-permute-done | bytes 473232 | tf_op jit(solution)/shard_map/ppermute | solution.py:21
  58.8 7.8 %pad_maximum_fusion = f32[7,6,130,130]{3,2,1,0:T(8,128)S(1)} fusion(f32[7,1,130,130]{3,2,1,0:T(8,128)S(1)} %copy.74, f32[7,4,130,1]{3,2,1,0:T(8,128)S(1)} %copy-done.2, f32[7,4,1,128]{3,2,1,0:T(1,128)} %bitcast.4, f32[1,4,128,128]{3,2,1,0:T(8,128)S(1)} %bitcast.66, f32[3,4,128,128]{3,2,1,0:T(8,128)S(1)} %copy-done.1, f32[3,4,128,128]{3,2,1,0:T(8,128)S(1)} %copy-done, ...), kind=kLoop, calls=%fused_computation | loop fusion | flops 5678400 | bytes 5678400 | tf_op jit(solution)/shard_map/concatenate | solution.py:17
  67.1 2.2 %multiply_multiply_fusion.3 = (f32[5,129,129]{2,1,0:T(8,128)S(1)}, f32[5,129,129]{2,1,0:T(8,128)S(1)}) fusion(f32[6,130,130]{2,1,0:T(8,128)S(1)} %get-tuple-element.16, f32[6,130,130]{2,1,0:T(8,128)S(1)} %get-tuple-element.17, f32[6,130,130]{2,1,0:T(8,128)S(1)} %get-tuple-element.11, f32[6,130,130]{2,1,0:T(8,128)S(1)} %get-tuple-element.15, ...), kind=kLoop, calls=%fused_computation.7 | loop fusion | flops 1331280 | bytes 4995396 | tf_op jit(solution)/shard_map/mul | solution.py:92
  72.1 3.2 %collective-permute-start.6 = (f32[3,4,1,128]{3,1,2,0:T(4,128)S(1)}, f32[3,4,1,128]{3,1,2,0:T(4,128)S(1)}, u32[]{:S(2)}, u32[]{:S(2)}) collective-permute-start(f32[3,4,1,128]{3,1,2,0:T(4,128)S(1)} %bitcast.86), channel_id=1, source_target_pairs={{0,8},{8,16},{16,24},{1,9},{9,17},{17,25},{2,10},{10,18},{18,26},{... | collective-permute-start | bytes 18440 | tf_op jit(solution)/shard_map/ppermute | solution.py:19
  76.6 3.1 %collective-permute-done.7 = f32[3,4,1,128]{3,1,2,0:T(4,128)S(1)} collective-permute-done((f32[3,4,1,128]{3,1,2,0:T(4,128)S(1)}, f32[3,4,1,128]{3,1,2,0:T(4,128)S(1)}, u32[]{:S(2)}, u32[]{:S(2)}) %collective-permute-start.7) | collective-permute-done | bytes 6176 | tf_op jit(solution)/shard_map/ppermute | solution.py:21
  84.1 2.8 %collective-permute-done.9 = f32[3,4,130,1]{2,1,3,0:T(4,128)S(1)} collective-permute-done((f32[3,4,130,1]{2,1,3,0:T(4,128)S(1)}, f32[3,4,130,1]{2,1,3,0:T(4,128)S(1)}, u32[]{:S(2)}, u32[]{:S(2)}) %collective-permute-start.9) | collective-permute-done | bytes 6272 | tf_op jit(solution)/shard_map/ppermute | solution.py:21
  87.7 4.6 %collective-permute-start.10 = (f32[3,1,130,130]{3,2,1,0:T(8,128)S(1)}, f32[3,1,130,130]{3,2,1,0:T(8,128)S(1)}, u32[]{:S(2)}, u32[]{:S(2)}) collective-permute-start(f32[3,1,130,130]{3,2,1,0:T(8,128)S(1)} %get-tuple-element.28), channel_id=1, source_target_pairs={{0,1},{1,2},{2,3},{4,5},{5,6},{6,7},{8,9},{9,10},{10,11},{12,13},{... | collective-permute-start | bytes 608408 | tf_op jit(solution)/shard_map/ppermute | solution.py:19
  92.3 1.9 %collective-permute-start.11 = (f32[3,1,130,130]{3,2,1,0:T(8,128)S(1)}, f32[3,1,130,130]{3,2,1,0:T(8,128)S(1)}, u32[]{:S(2)}, u32[]{:S(2)}) collective-permute-start(f32[3,1,130,130]{3,2,1,0:T(8,128)S(1)} %get-tuple-element.29), channel_id=1, source_target_pairs={{1,0},{2,1},{3,2},{5,4},{6,5},{7,6},{9,8},{10,9},{11,10},{13,12},{... | collective-permute-start | bytes 608408 | tf_op jit(solution)/shard_map/ppermute | solution.py:21
  94.2 3.0 %collective-permute-done.10 = f32[3,1,130,130]{3,2,1,0:T(8,128)S(1)} collective-permute-done((f32[3,1,130,130]{3,2,1,0:T(8,128)S(1)}, f32[3,1,130,130]{3,2,1,0:T(8,128)S(1)}, u32[]{:S(2)}, u32[]{:S(2)}) %collective-permute-start.10) | collective-permute-done | bytes 202832 | tf_op jit(solution)/shard_map/ppermute | solution.py:19
  97.3 4.4 %collective-permute-done.11 = f32[3,1,130,130]{3,2,1,0:T(8,128)S(1)} collective-permute-done((f32[3,1,130,130]{3,2,1,0:T(8,128)S(1)}, f32[3,1,130,130]{3,2,1,0:T(8,128)S(1)}, u32[]{:S(2)}, u32[]{:S(2)}) %collective-permute-start.11) | collective-permute-done | bytes 202832 | tf_op jit(solution)/shard_map/ppermute | solution.py:21
  106.9 3.2 %collective-permute-start.12 = (f32[3,4,1,128]{3,1,2,0:T(4,128)S(1)}, f32[3,4,1,128]{3,1,2,0:T(4,128)S(1)}, u32[]{:S(2)}, u32[]{:S(2)}) collective-permute-start(f32[3,4,1,128]{3,1,2,0:T(4,128)S(1)} %bitcast.87), channel_id=1, source_target_pairs={{0,8},{8,16},{16,24},{1,9},{9,17},{17,25},{2,10},{10,18},{18,26},{... | collective-permute-start | bytes 18440 | tf_op jit(solution)/shard_map/ppermute | solution.py:19
  111.7 2.8 %collective-permute-done.13 = f32[3,4,1,128]{3,1,2,0:T(4,128)S(1)} collective-permute-done((f32[3,4,1,128]{3,1,2,0:T(4,128)S(1)}, f32[3,4,1,128]{3,1,2,0:T(4,128)S(1)}, u32[]{:S(2)}, u32[]{:S(2)}) %collective-permute-start.13) | collective-permute-done | bytes 6176 | tf_op jit(solution)/shard_map/ppermute | solution.py:21
  118.8 2.8 %collective-permute-done.15 = f32[3,4,130,1]{2,1,3,0:T(4,128)S(1)} collective-permute-done((f32[3,4,130,1]{2,1,3,0:T(4,128)S(1)}, f32[3,4,130,1]{2,1,3,0:T(4,128)S(1)}, u32[]{:S(2)}, u32[]{:S(2)}) %collective-permute-start.15) | collective-permute-done | bytes 6272 | tf_op jit(solution)/shard_map/ppermute | solution.py:21
  122.4 4.6 %collective-permute-start.16 = (f32[3,1,130,130]{3,2,1,0:T(8,128)S(1)}, f32[3,1,130,130]{3,2,1,0:T(8,128)S(1)}, u32[]{:S(2)}, u32[]{:S(2)}) collective-permute-start(f32[3,1,130,130]{3,2,1,0:T(8,128)S(1)} %get-tuple-element.26), channel_id=1, source_target_pairs={{0,1},{1,2},{2,3},{4,5},{5,6},{6,7},{8,9},{9,10},{10,11},{12,13},{... | collective-permute-start | bytes 608408 | tf_op jit(solution)/shard_map/ppermute | solution.py:19
  127.0 1.9 %collective-permute-start.17 = (f32[3,1,130,130]{3,2,1,0:T(8,128)S(1)}, f32[3,1,130,130]{3,2,1,0:T(8,128)S(1)}, u32[]{:S(2)}, u32[]{:S(2)}) collective-permute-start(f32[3,1,130,130]{3,2,1,0:T(8,128)S(1)} %get-tuple-element.27), channel_id=1, source_target_pairs={{1,0},{2,1},{3,2},{5,4},{6,5},{7,6},{9,8},{10,9},{11,10},{13,12},{... | collective-permute-start | bytes 608408 | tf_op jit(solution)/shard_map/ppermute | solution.py:21
  128.9 3.0 %collective-permute-done.16 = f32[3,1,130,130]{3,2,1,0:T(8,128)S(1)} collective-permute-done((f32[3,1,130,130]{3,2,1,0:T(8,128)S(1)}, f32[3,1,130,130]{3,2,1,0:T(8,128)S(1)}, u32[]{:S(2)}, u32[]{:S(2)}) %collective-permute-start.16) | collective-permute-done | bytes 202832 | tf_op jit(solution)/shard_map/ppermute | solution.py:19
  132.0 4.4 %collective-permute-done.17 = f32[3,1,130,130]{3,2,1,0:T(8,128)S(1)} collective-permute-done((f32[3,1,130,130]{3,2,1,0:T(8,128)S(1)}, f32[3,1,130,130]{3,2,1,0:T(8,128)S(1)}, u32[]{:S(2)}, u32[]{:S(2)}) %collective-permute-start.17) | collective-permute-done | bytes 202832 | tf_op jit(solution)/shard_map/ppermute | solution.py:21
  138.4 1.8 %add_multiply_fusion = (f32[4,128,128]{2,1,0:T(8,128)}, f32[1,4,128,128]{3,2,1,0:T(8,128)S(1)}, f32[1,4,128,128]{3,2,1,0:T(8,128)S(1)}, f32[1,4,128,128]{3,2,1,0:T(8,128)S(1)}) fusion(f32[5,129,129]{2,1,0:T(8,128)S(1)} %multiply_multiply_fusion, f32[5,129,129]{2,1,0:T(8,128)} %copy-done.5), kind=kLoop, calls=%fused_computation.99 | loop fusion | flops 458752 | bytes 2359296 | tf_op jit(solution)/shard_map/add | solution.py:105
  (108 shorter events, 33.5 us)
Async XLA Ops:
  1.6 5.3 %collective-permute-start = (f32[7,4,1,128]{3,1,2,0:T(4,128)S(1)}, f32[7,4,1,128]{3,1,2,0:T(4,128)S(1)}, u32[]{:S(2)}, u32[]{:S(2)}) collective-permute-start(f32[7,4,1,128]{3,1,2,0:T(4,128)S(1)} %bitcast.83), channel_id=1, source_target_pairs={{0,8},{8,16},{16,24},{1,9},{9,17},{17,25},{2,10},{10,18},{18,26},{... | collective-permute-start | bytes 43016 | tf_op jit(solution)/shard_map/ppermute | solution.py:19
  5.6 4.6 %collective-permute-start.1 = (f32[7,4,1,128]{3,1,2,0:T(4,128)S(1)}, f32[7,4,1,128]{3,1,2,0:T(4,128)}, u32[]{:S(2)}, u32[]{:S(2)}) collective-permute-start(f32[7,4,1,128]{3,1,2,0:T(4,128)S(1)} %bitcast.82), channel_id=1, source_target_pairs={{8,0},{16,8},{24,16},{9,1},{17,9},{25,17},{10,2},{18,10},{26,18},{... | collective-permute-start | bytes 43016 | tf_op jit(solution)/shard_map/ppermute | solution.py:21
  16.9 6.7 %collective-permute-start.2 = (f32[7,4,130,1]{2,1,3,0:T(4,128)}, f32[7,4,130,1]{2,1,3,0:T(4,128)}, u32[]{:S(2)}, u32[]{:S(2)}) collective-permute-start(f32[7,4,130,1]{2,1,3,0:T(4,128)} %copy.67), channel_id=1, source_target_pairs={{0,4},{1,5},{2,6},{3,7},{8,12},{9,13},{10,14},{11,15},{16,20},{17,... | collective-permute-start | bytes 43688 | tf_op jit(solution)/shard_map/ppermute | solution.py:19
  20.6 9.3 %copy-start = (f32[3,4,128,128]{3,2,1,0:T(8,128)S(1)}, f32[3,4,128,128]{3,2,1,0:T(8,128)}, u32[]{:S(2)}) copy-start(f32[3,4,128,128]{3,2,1,0:T(8,128)} %param.7) | copy-start | bytes 2359300
  20.6 9.3 %copy-start.1 = (f32[3,4,128,128]{3,2,1,0:T(8,128)S(1)}, f32[3,4,128,128]{3,2,1,0:T(8,128)}, u32[]{:S(2)}) copy-start(f32[3,4,128,128]{3,2,1,0:T(8,128)} %param.8) | copy-start | bytes 2359300
  22.3 4.9 %collective-permute-start.3 = (f32[7,4,130,1]{2,1,3,0:T(4,128)}, f32[7,4,130,1]{2,1,3,0:T(4,128)}, u32[]{:S(2)}, u32[]{:S(2)}) collective-permute-start(f32[7,4,130,1]{2,1,3,0:T(4,128)} %copy.68), channel_id=1, source_target_pairs={{4,0},{5,1},{6,2},{7,3},{12,8},{13,9},{14,10},{15,11},{20,16},{21,... | collective-permute-start | bytes 43688 | tf_op jit(solution)/shard_map/ppermute | solution.py:21
  33.9 17.4 %collective-permute-start.4 = (f32[7,1,130,130]{3,1,2,0:T(1,128)}, f32[7,1,130,130]{3,1,2,0:T(1,128)}, u32[]{:S(2)}, u32[]{:S(2)}) collective-permute-start(f32[7,1,130,130]{3,1,2,0:T(1,128)} %copy.71), channel_id=1, source_target_pairs={{0,1},{1,2},{2,3},{4,5},{5,6},{6,7},{8,9},{9,10},{10,11},{12,13},{... | collective-permute-start | bytes 1419608 | tf_op jit(solution)/shard_map/ppermute | solution.py:19
  42.4 15.2 %collective-permute-start.5 = (f32[7,1,130,130]{3,1,2,0:T(1,128)}, f32[7,1,130,130]{3,1,2,0:T(1,128)}, u32[]{:S(2)}, u32[]{:S(2)}) collective-permute-start(f32[7,1,130,130]{3,1,2,0:T(1,128)} %copy.72), channel_id=1, source_target_pairs={{1,0},{2,1},{3,2},{5,4},{6,5},{7,6},{9,8},{10,9},{11,10},{13,12},{... | collective-permute-start | bytes 1419608 | tf_op jit(solution)/shard_map/ppermute | solution.py:21
  44.5 14.3 %copy-start.2 = (f32[7,4,130,1]{3,2,1,0:T(8,128)S(1)}, f32[7,4,130,1]{3,2,1,0:T(8,128)}, u32[]{:S(2)}) copy-start(f32[7,4,130,1]{3,2,1,0:T(8,128)} %copy.70) | copy-start | bytes 43684
  44.5 14.3 %copy-start.6 = (f32[4,128,128]{2,1,0:T(8,128)S(1)}, f32[4,128,128]{2,1,0:T(8,128)}, u32[]{:S(2)}) copy-start(f32[4,128,128]{2,1,0:T(8,128)} %param.5) | copy-start | bytes 786436
  44.6 22.6 %copy-start.23 = (f32[129]{0:T(256)}, f32[129]{0:T(256)S(1)}, u32[]{:S(2)}) copy-start(f32[129]{0:T(256)S(1)} %and_select_fusion) | copy-start | bytes 1552
  69.6 1.3 copy-start.7
  70.3 1.6 %copy-start.11 = (f32[4,128,128]{2,1,0:T(8,128)}, f32[4,128,128]{2,1,0:T(8,128)S(1)}, u32[]{:S(2)}) copy-start(f32[4,128,128]{2,1,0:T(8,128)S(1)} %multiply_reduce_fusion.3) | copy-start | bytes 786436
  72.1 4.5 %collective-permute-start.6 = (f32[3,4,1,128]{3,1,2,0:T(4,128)S(1)}, f32[3,4,1,128]{3,1,2,0:T(4,128)S(1)}, u32[]{:S(2)}, u32[]{:S(2)}) collective-permute-start(f32[3,4,1,128]{3,1,2,0:T(4,128)S(1)} %bitcast.86), channel_id=1, source_target_pairs={{0,8},{8,16},{16,24},{1,9},{9,17},{17,25},{2,10},{10,18},{18,26},{... | collective-permute-start | bytes 18440 | tf_op jit(solution)/shard_map/ppermute | solution.py:19
  75.3 4.4 %collective-permute-start.7 = (f32[3,4,1,128]{3,1,2,0:T(4,128)S(1)}, f32[3,4,1,128]{3,1,2,0:T(4,128)S(1)}, u32[]{:S(2)}, u32[]{:S(2)}) collective-permute-start(f32[3,4,1,128]{3,1,2,0:T(4,128)S(1)} %bitcast.84), channel_id=1, source_target_pairs={{8,0},{16,8},{24,16},{9,1},{17,9},{25,17},{10,2},{18,10},{26,18},{... | collective-permute-start | bytes 18440 | tf_op jit(solution)/shard_map/ppermute | solution.py:21
  80.5 3.3 %collective-permute-start.8 = (f32[3,4,130,1]{2,1,3,0:T(4,128)S(1)}, f32[3,4,130,1]{2,1,3,0:T(4,128)S(1)}, u32[]{:S(2)}, u32[]{:S(2)}) collective-permute-start(f32[3,4,130,1]{2,1,3,0:T(4,128)S(1)} %copy.83), channel_id=1, source_target_pairs={{0,4},{1,5},{2,6},{3,7},{8,12},{9,13},{10,14},{11,15},{16,20},{17,... | collective-permute-start | bytes 18728 | tf_op jit(solution)/shard_map/ppermute | solution.py:19
  82.5 4.4 %collective-permute-start.9 = (f32[3,4,130,1]{2,1,3,0:T(4,128)S(1)}, f32[3,4,130,1]{2,1,3,0:T(4,128)S(1)}, u32[]{:S(2)}, u32[]{:S(2)}) collective-permute-start(f32[3,4,130,1]{2,1,3,0:T(4,128)S(1)} %copy.84), channel_id=1, source_target_pairs={{4,0},{5,1},{6,2},{7,3},{12,8},{13,9},{14,10},{15,11},{20,16},{21,... | collective-permute-start | bytes 18728 | tf_op jit(solution)/shard_map/ppermute | solution.py:21
  87.7 9.6 %collective-permute-start.10 = (f32[3,1,130,130]{3,2,1,0:T(8,128)S(1)}, f32[3,1,130,130]{3,2,1,0:T(8,128)S(1)}, u32[]{:S(2)}, u32[]{:S(2)}) collective-permute-start(f32[3,1,130,130]{3,2,1,0:T(8,128)S(1)} %get-tuple-element.28), channel_id=1, source_target_pairs={{0,1},{1,2},{2,3},{4,5},{5,6},{6,7},{8,9},{9,10},{10,11},{12,13},{... | collective-permute-start | bytes 608408 | tf_op jit(solution)/shard_map/ppermute | solution.py:19
  92.3 9.4 %collective-permute-start.11 = (f32[3,1,130,130]{3,2,1,0:T(8,128)S(1)}, f32[3,1,130,130]{3,2,1,0:T(8,128)S(1)}, u32[]{:S(2)}, u32[]{:S(2)}) collective-permute-start(f32[3,1,130,130]{3,2,1,0:T(8,128)S(1)} %get-tuple-element.29), channel_id=1, source_target_pairs={{1,0},{2,1},{3,2},{5,4},{6,5},{7,6},{9,8},{10,9},{11,10},{13,12},{... | collective-permute-start | bytes 608408 | tf_op jit(solution)/shard_map/ppermute | solution.py:21
  103.1 1.3 copy-start.4
  103.1 1.3 copy-start.8
  103.1 1.3 copy-start.10
  103.1 1.3 copy-start.13
  103.2 1.4 copy-start.16
  104.4 1.3 copy-start.22
  106.9 4.7 %collective-permute-start.12 = (f32[3,4,1,128]{3,1,2,0:T(4,128)S(1)}, f32[3,4,1,128]{3,1,2,0:T(4,128)S(1)}, u32[]{:S(2)}, u32[]{:S(2)}) collective-permute-start(f32[3,4,1,128]{3,1,2,0:T(4,128)S(1)} %bitcast.87), channel_id=1, source_target_pairs={{0,8},{8,16},{16,24},{1,9},{9,17},{17,25},{2,10},{10,18},{18,26},{... | collective-permute-start | bytes 18440 | tf_op jit(solution)/shard_map/ppermute | solution.py:19
  110.1 4.4 %collective-permute-start.13 = (f32[3,4,1,128]{3,1,2,0:T(4,128)S(1)}, f32[3,4,1,128]{3,1,2,0:T(4,128)S(1)}, u32[]{:S(2)}, u32[]{:S(2)}) collective-permute-start(f32[3,4,1,128]{3,1,2,0:T(4,128)S(1)} %bitcast.85), channel_id=1, source_target_pairs={{8,0},{16,8},{24,16},{9,1},{17,9},{25,17},{10,2},{18,10},{26,18},{... | collective-permute-start | bytes 18440 | tf_op jit(solution)/shard_map/ppermute | solution.py:21
  115.4 3.1 %collective-permute-start.14 = (f32[3,4,130,1]{2,1,3,0:T(4,128)S(1)}, f32[3,4,130,1]{2,1,3,0:T(4,128)S(1)}, u32[]{:S(2)}, u32[]{:S(2)}) collective-permute-start(f32[3,4,130,1]{2,1,3,0:T(4,128)S(1)} %copy.95), channel_id=1, source_target_pairs={{0,4},{1,5},{2,6},{3,7},{8,12},{9,13},{10,14},{11,15},{16,20},{17,... | collective-permute-start | bytes 18728 | tf_op jit(solution)/shard_map/ppermute | solution.py:19
  117.2 4.4 %collective-permute-start.15 = (f32[3,4,130,1]{2,1,3,0:T(4,128)S(1)}, f32[3,4,130,1]{2,1,3,0:T(4,128)S(1)}, u32[]{:S(2)}, u32[]{:S(2)}) collective-permute-start(f32[3,4,130,1]{2,1,3,0:T(4,128)S(1)} %copy.96), channel_id=1, source_target_pairs={{4,0},{5,1},{6,2},{7,3},{12,8},{13,9},{14,10},{15,11},{20,16},{21,... | collective-permute-start | bytes 18728 | tf_op jit(solution)/shard_map/ppermute | solution.py:21
  122.4 9.6 %collective-permute-start.16 = (f32[3,1,130,130]{3,2,1,0:T(8,128)S(1)}, f32[3,1,130,130]{3,2,1,0:T(8,128)S(1)}, u32[]{:S(2)}, u32[]{:S(2)}) collective-permute-start(f32[3,1,130,130]{3,2,1,0:T(8,128)S(1)} %get-tuple-element.26), channel_id=1, source_target_pairs={{0,1},{1,2},{2,3},{4,5},{5,6},{6,7},{8,9},{9,10},{10,11},{12,13},{... | collective-permute-start | bytes 608408 | tf_op jit(solution)/shard_map/ppermute | solution.py:19
  127.0 9.4 %collective-permute-start.17 = (f32[3,1,130,130]{3,2,1,0:T(8,128)S(1)}, f32[3,1,130,130]{3,2,1,0:T(8,128)S(1)}, u32[]{:S(2)}, u32[]{:S(2)}) collective-permute-start(f32[3,1,130,130]{3,2,1,0:T(8,128)S(1)} %get-tuple-element.27), channel_id=1, source_target_pairs={{1,0},{2,1},{3,2},{5,4},{6,5},{7,6},{9,8},{10,9},{11,10},{13,12},{... | collective-permute-start | bytes 608408 | tf_op jit(solution)/shard_map/ppermute | solution.py:21
  137.3 2.9 %copy-start.14 = (f32[4,128,128]{2,1,0:T(8,128)S(1)}, f32[4,128,128]{2,1,0:T(8,128)}, u32[]{:S(2)}) copy-start(f32[4,128,128]{2,1,0:T(8,128)} %get-tuple-element.60) | copy-start | bytes 786436
  (11 other events, 12.0 us)
where the time goes:
time: 142 us; the launch traced here: 141 us
  starting transfers between devices  46.7 us (33%)
  waiting for transfers between devices  43.5 us (31%)
  other arithmetic  25.6 us (18%)
  local copies, waits for them, and re-layouts  24.2 us (17%)
    ppermute x9, starting transfers between devices, extended(): lax.ppermute(tail, axis, [(i, (i + 1) % count) for i in range(ends)])  32.8 us
    ppermute x9, waiting for transfers between devices, extended(): lax.ppermute(head, axis, [((i + 1) % count, i) for i in range(ends)])  30.8 us
    ppermute x9, starting transfers between devices, extended(): lax.ppermute(head, axis, [((i + 1) % count, i) for i in range(ends)])  13.9 us
    ppermute x9, waiting for transfers between devices, extended(): lax.ppermute(tail, axis, [(i, (i + 1) % count) for i in range(ends)])  12.7 us
    concatenate x6, other arithmetic, extended(): jnp.concatenate([lax.ppermute(tail, axis, [(i, (i + 1) % count) for i in...  11.1 us
    slice x9, local copies, waits for them, and re-layouts, extended(): lax.slice_in_dim(cells, cells.shape[dim] - width, cells.shape[dim], axis=...  8.55 us
    ppermute x4, local copies, waits for them, and re-layouts, extended(): lax.ppermute(head, axis, [((i + 1) % count, i) for i in range(ends)])  4.65 us
    slice x4, local copies, waits for them, and re-layouts, extended(): head = lax.slice_in_dim(cells, 0, width, axis=dim)  4.5 us
  transfers between devices with their start and end apart: 18, of which 12 were waited for; matrix products, arithmetic and copies ran while one was open for 6% of the time, Pallas kernels for 0%

commit v1 on v0

v1 whole, which is shorter than its diff:
```python
import functools

import jax
import jax.numpy as jnp
from jax import lax
from jax.experimental import pallas as pl
from jax.experimental.pallas import tpu as pltpu
from jax.sharding import PartitionSpec as P

STEP = 0.08
INVERSE = 0.5
SMOOTH = 0.01

AFTER = (3, 3, 3, 2, 2, 2, 2, 2, 2, 2, 3)
BEFORE = (2, 3, 2, 1, 2, 1, 2, 2, 2, 2, 2)
FIELDS = len(AFTER)
WEIGHT, DATA = 9, 10
PAD = 16
SUB = 8
LANES = 128
GROUP = 16


class Link:
    def __init__(self, axis, count):
        place = lax.axis_index(axis)
        self.even = lax.rem(place, 2) == 0
        self.odd = jnp.logical_not(self.even)
        self.before = place > 0
        self.after = place < count - 1


def phases(count):
    return 1 if count == 2 else 2


def swap(values, axis, count, spare, spare_count):
    out = [lax.all_gather(values[0], axis, axis_index_groups=[[i, i + 1] for i in range(0, count, 2)])]
    if count > 2:
        at = lambda i, j: i * spare_count + j
        groups = [[at(i, j), at(i + 1, j)] for i in range(1, count - 1, 2) for j in range(spare_count)]
        groups += [[at(i, j), at(i, j + 1)] for i in (0, count - 1) for j in range(0, spare_count, 2)]
        out.append(lax.all_gather(values[1], (axis, spare), axis_index_groups=groups))
    return out


def send(link, outs, up, down):
    @pl.when(link.even)
    def _():
        up(outs[0])
        if len(outs) > 1:
            down(outs[1])

    @pl.when(link.odd)
    def _():
        down(outs[0])
        if len(outs) > 1:
            up(outs[1])


def receive(link, ins, before, after):
    pl.when(link.odd)(lambda: before(ins[0].at[0]))
    pl.when(link.even)(lambda: after(ins[0].at[1]))
    if len(ins) > 1:
        pl.when(jnp.logical_and(link.even, link.before))(lambda: before(ins[1].at[0]))
        pl.when(jnp.logical_and(link.odd, link.after))(lambda: after(ins[1].at[1]))
    pl.when(jnp.logical_not(link.before))(lambda: before(None))
    pl.when(jnp.logical_not(link.after))(lambda: after(None))


def lane_ids():
    return lax.broadcasted_iota(jnp.int32, (SUB, LANES), 1)


def turn(x, by):
    return pltpu.roll(x, by % LANES if isinstance(by, int) else lax.rem(by + 4 * LANES, LANES), 1)


def col_before(x, strip, k, lane):
    return jnp.where(lane == 0, turn(strip, -(GROUP * (k + 1) + 11)), turn(x, 1))


def col_after(x, strip, k, lane):
    return jnp.where(lane == LANES - 1, turn(strip, LANES - 1 - (GROUP * (k + 1) + 4)), turn(x, -1))


def sources(dm, ds, ct, w, d):
    return [(r, a) for r in (dm, ds, ct) for a in range(3)] + [(w, None), (d, None)]


def src_rows(source, k, rows):
    ref, a = source
    return ref[k, rows, :] if a is None else ref[a, k, rows, :]


def offsets():
    out, total = [], 0
    for f in range(FIELDS):
        out.append(total)
        total += AFTER[f]
    return out, total


def rows_out(counts, dm, ds, ct, w, d, *outs):
    planes, rows = d.shape[0], d.shape[1]
    src = sources(dm, ds, ct, w, d)
    offs, per = offsets()
    link = Link("gx", counts["gx"])

    def up(out):
        for f in range(FIELDS):
            for k in range(planes):
                out[pl.ds(per * k + offs[f], BEFORE[f]), :] = src_rows(src[f], k, pl.ds(rows - BEFORE[f], BEFORE[f]))

    def down(out):
        for f in range(FIELDS):
            for k in range(planes):
                out[pl.ds(per * k + offs[f], AFTER[f]), :] = src_rows(src[f], k, pl.ds(0, AFTER[f]))

    send(link, outs, up, down)


def slot(f):
    return f // 8, 4 * (f % 4) + 64 * ((f // 4) % 2)


def build(counts, dm, ds, ct, w, d, *refs):
    planes, rows = d.shape[0], d.shape[1]
    nx, ny = phases(counts["gx"]), phases(counts["gy"])
    got, (em, es), outs = refs[:nx], refs[nx : nx + 2], refs[nx + 2 :]
    src = sources(dm, ds, ct, w, d)
    offs, per = offsets()
    lane = lane_ids()

    def halo(start, counted, deep):
        def fill(ref):
            for f in range(FIELDS):
                for k in range(planes):
                    if ref is None:
                        at, many = start(deep), deep
                        value = jnp.full((deep, LANES), 1.0 if f == WEIGHT else 0.0, jnp.float32)
                    else:
                        at, many = start(counted[f]), counted[f]
                        value = ref[pl.ds(per * k + offs[f], many), :]
                    em[f, k, pl.ds(at, many), :] = value

        return fill

    receive(
        Link("gx", counts["gx"]),
        got,
        halo(lambda n: PAD - n, BEFORE, 3),
        halo(lambda n: PAD + rows, AFTER, 3),
    )
    link = Link("gy", counts["gy"])
    part = lax.rem(lane, GROUP) // 4
    plane_of = lane // GROUP

    def tile(row, read):
        packed = [[None, None] for _ in range(ny)]
        for f in range(FIELDS):
            strip = jnp.full((SUB, LANES), 1.0 if f == WEIGHT else 0.0, jnp.float32)
            for k in range(planes):
                x = read(f, k)
                base = GROUP * (k + 1)
                here = plane_of == k + 1
                strip = jnp.where(jnp.logical_and(here, part == 0), turn(x, base + 4), strip)
                strip = jnp.where(jnp.logical_and(here, part == 3), turn(x, base + 12), strip)
            es[f, pl.ds(row, SUB), :] = strip
            which, shift = slot(f)
            mask = jnp.logical_and(part == (f % 4), lane // 64 == (f // 4) % 2)
            for p in range(ny):
                up = link.even if p == 0 else link.odd
                moved = turn(strip, shift - GROUP + jnp.where(up, 0, -12))
                old = packed[p][which]
                packed[p][which] = moved if old is None else jnp.where(mask, moved, old)
        for p in range(ny):
            for which in range(2):
                outs[p][which, pl.ds(row - SUB, SUB), :] = packed[p][which]

    @pl.loop(0, rows // SUB)
    def _(t):
        inside = pl.multiple_of(t * SUB, SUB)
        row = pl.multiple_of(t * SUB + PAD, SUB)

        def read(f, k):
            x = src_rows(src[f], k, pl.ds(inside, SUB))
            em[f, k, pl.ds(row, SUB), :] = x
            return x

        tile(row, read)

    @pl.loop(0, 2)
    def _(t):
        row = pl.multiple_of(PAD - SUB + t * (rows + SUB), SUB)
        tile(row, lambda f, k: em[f, k, pl.ds(row, SUB), :])


def fold(strip, group, out, base, tiles):
    lane = lane_ids()
    many = LANES // GROUP

    @pl.loop(0, tiles)
    def _(t):
        side = lax.rem(t, many)
        at = pl.ds(pl.multiple_of(base + SUB * (t // many), SUB), SUB)
        x = strip[pl.ds(pl.multiple_of(SUB * t + SUB, SUB), SUB), :]
        out[at, :] = jnp.where(lane // GROUP == side, turn(x, GROUP * (side - group)), out[at, :])


def unfold(ref, base, t, group):
    many = LANES // GROUP
    x = ref[pl.ds(pl.multiple_of(base + SUB * (t // many), SUB), SUB), :]
    return turn(x, GROUP * (group - lax.rem(t, many)))


def sizes(rows):
    tiles = (rows + 2 * PAD - 2 * SUB) // SUB
    folded = SUB * pl.cdiv(tiles * GROUP, LANES)
    return tiles, SUB * tiles, folded


def copy_rows(src, out, base, tiles):
    @pl.loop(0, tiles)
    def _(t):
        out[pl.ds(pl.multiple_of(base + SUB * t, SUB), SUB), :] = src[pl.ds(pl.multiple_of(SUB * t + SUB, SUB), SUB), :]


def plane_out(link, outs, up, down, planes, rows):
    tiles, flat, folded = sizes(rows)

    def put(items, group):
        def write(out):
            for i, (plane, strip) in enumerate(items):
                base = i * (flat + folded)
                copy_rows(plane, out, base, tiles)
                fold(strip, group, out, base + flat, tiles)

        return write

    send(link, outs, put(up, planes), put(down, 1))


def plane_in(link, ins, below, above):
    def put(dst):
        def fill(ref):
            @pl.loop(0, dst.shape[0] // SUB)
            def _(t):
                at = pl.ds(pl.multiple_of(t * SUB, SUB), SUB)
                dst[at, :] = jnp.zeros((SUB, LANES), jnp.float32) if ref is None else ref[at, :]

        return fill

    receive(link, ins, put(below), put(above))


def strips_and_values(counts, em, es, *refs):
    planes, rows = em.shape[1], em.shape[2] - 2 * PAD
    ny = phases(counts["gy"])
    got, (full, v, vs), outs = refs[:ny], refs[ny : ny + 3], refs[ny + 3 :]
    link = Link("gy", counts["gy"])
    row_link = Link("gx", counts["gx"])
    lane = lane_ids()
    part = lax.rem(lane, GROUP) // 4
    near = jnp.logical_or(part == 1, part == 2)
    real_after = jnp.logical_and(part == 1, link.after)
    real_before = jnp.logical_and(part == 2, link.before)
    lost = jnp.logical_and(part == 1, jnp.logical_not(link.after))
    inner = lane // GROUP >= 2
    tiles, flat, folded = sizes(rows)

    @pl.loop(0, tiles)
    def _(t):
        row = pl.multiple_of(SUB * t + SUB, SUB)
        at = pl.ds(pl.multiple_of(SUB * t, SUB), SUB)

        def sent(which, index):
            if ny == 1:
                return got[0][index, which, at, :]
            first = link.odd if index == 0 else link.even
            return jnp.where(first, got[0][index, which, at, :], got[1][index, which, at, :])

        blocks = [[sent(which, index) for which in range(2)] for index in range(2)]
        for f in range(FIELDS):
            which, shift = slot(f)
            x = jnp.where(near, 1.0 if f == WEIGHT else 0.0, es[f, pl.ds(row, SUB), :])
            x = jnp.where(real_after, turn(blocks[1][which], GROUP + 4 - shift), x)
            x = jnp.where(real_before, turn(blocks[0][which], GROUP + 8 - shift), x)
            full[f, pl.ds(row, SUB), :] = x

    @pl.loop(0, tiles)
    def _(t):
        row = pl.multiple_of(SUB * t + SUB, SUB)
        at, lower = pl.ds(row, SUB), pl.ds(row - 1, SUB)
        keep = jnp.logical_or(t < tiles - 1, row_link.after)
        for m in range(2):
            p0, p1, p2 = 3 * m, 3 * m + 1, 3 * m + 2
            s0, s2 = full[p0, at, :], full[p2, at, :]
            x = s0 - jnp.where(inner, turn(s0, GROUP), 0.0)
            x = x + (full[p1, at, :] - full[p1, lower, :])
            x = x + (s2 - turn(s2, 1))
            x = x - INVERSE * full[DATA, at, :]
            vs[m, at, :] = jnp.where(keep, jnp.where(lost, 0.0, x), 0.0)
            last = None
            for k in range(planes):
                x = now = em[p0, k, at, :]
                if k:
                    x = x - last
                last = now
                x = x + (em[p1, k, at, :] - em[p1, k, lower, :])
                y = em[p2, k, at, :]
                x = x + (y - col_before(y, s2, k, lane))
                x = x - INVERSE * em[DATA, k, at, :]
                v[m, k, at, :] = jnp.where(keep, x, 0.0)

    plane_out(
        Link("gz", counts["gz"]),
        outs,
        [(em.at[3 * m, planes - 1], full.at[3 * m]) for m in range(2)],
        [(v.at[m, 0], vs.at[m]) for m in range(2)],
        planes,
        rows,
    )


def settle(first, strip, last, last_strip, below, above, base, has_after, out_first, out_ghost, out_strip, planes, rows):
    tiles, flat, folded = sizes(rows)
    lane = lane_ids()
    group = lane // GROUP

    @pl.loop(0, tiles)
    def _(t):
        at = pl.ds(pl.multiple_of(SUB * t + SUB, SUB), SUB)
        sent = pl.ds(pl.multiple_of(base + SUB * t, SUB), SUB)
        out_first[at, :] = first[at, :] - below[sent, :]
        out_ghost[at, :] = jnp.where(has_after, above[sent, :] - last[at, :], 0.0)
        x = strip[at, :]
        x = jnp.where(group == 1, x - unfold(below, base + flat, t, 1), x)
        ghost = unfold(above, base + flat, t, planes + 1) - turn(last_strip[at, :], GROUP)
        ghost = jnp.where(has_after, ghost, 0.0)
        out_strip[at, :] = jnp.where(group == planes + 1, ghost, x)


def pointwise(g, c, p, w):
    q = g[0] * g[0] + g[1] * g[1] + g[2] * g[2] + SMOOTH
    rn = lax.rsqrt(q)
    tn = STEP * (q * rn)
    rw = 1.0 / w
    rden = 1.0 / (1.0 + tn * rw)
    inner = c[0] * p[0] + c[1] * p[1] + c[2] * p[2]
    inner = inner + STEP * (c[0] * g[0] + c[1] * g[1] + c[2] * g[2])
    s = inner * rden * (rden * rw)
    wpart = s * (tn * rw)
    scale = STEP * rden
    along = (-STEP) * s * rn
    return [scale * c[a] + along * g[a] for a in range(3)], rden, wpart


class Around:
    def __init__(self, plane, strip, planes, row, lane):
        self.plane, self.planes, self.lane = plane, planes, lane
        self.at, self.upper = pl.ds(row, SUB), pl.ds(row + 1, SUB)
        self.strip = strip
        self.s = strip[self.at, :]
        self.now = [plane(k)[self.at, :] for k in range(planes + 1)]

    def steps(self, k):
        x = self.now[k]
        return (
            self.now[k + 1] - x,
            self.plane(k)[self.upper, :] - x,
            col_after(x, self.s, k, self.lane) - x,
        )

    def strip_steps(self):
        x = self.s
        return turn(x, -GROUP) - x, self.strip[self.upper, :] - x, turn(x, -1) - x


class Back:
    def __init__(self, rows_ref, strip_ref, row, lane):
        self.rows_ref, self.strip_ref, self.lane = rows_ref, strip_ref, lane
        self.at, self.lower = pl.ds(row, SUB), pl.ds(row - 1, SUB)
        self.last = None

    def strip(self, cg):
        self.s = cg[2]
        self.strip_ref[self.at, :] = cg[1]
        x = cg[0] - jnp.where(self.lane // GROUP >= 2, turn(cg[0], GROUP), 0.0)
        x = x + (cg[1] - self.strip_ref[self.lower, :])
        return x + (cg[2] - turn(cg[2], 1))

    def plane(self, k, cg):
        self.rows_ref[k, self.at, :] = cg[1]
        x = cg[0] if self.last is None else cg[0] - self.last
        self.last = cg[0]
        x = x + (cg[1] - self.rows_ref[k, self.lower, :])
        return x + (cg[2] - col_before(cg[2], self.s, k, self.lane))


def chooser(mid, first, ghost, planes):
    return lambda k: first if k == 0 else ghost if k == planes else mid.at[k]


def first_step(counts, em, full, v, vs, *refs):
    planes, rows = em.shape[1], em.shape[2] - 2 * PAD
    nz = phases(counts["gz"])
    got, refs = refs[:nz], refs[nz:]
    (r, rs, rd, rds, wp, top, tops), outs, scratch = refs[:7], refs[7 : 7 + nz], refs[7 + nz :]
    below, above, first, ghost, strip, rows_ref, strip_ref = scratch
    link, row_link, col_link = (Link(a, counts[a]) for a in ("gz", "gx", "gy"))
    lane = lane_ids()
    lost = jnp.logical_and(lax.rem(lane, GROUP) // 4 == 1, jnp.logical_not(col_link.after))
    tiles, flat, folded = sizes(rows)
    plane_in(link, got, below, above)
    settle(v.at[0, 0], vs.at[0], em.at[0, planes - 1], full.at[0], below, above, 0, link.after, first, ghost, strip, planes, rows)

    @pl.loop(0, tiles)
    def _(t):
        row = pl.multiple_of(SUB * t + SUB, SUB)
        at = pl.ds(row, SUB)
        keep = jnp.logical_or(t < tiles - 1, row_link.after)
        field = Around(chooser(v.at[0], first, ghost, planes), strip, planes, row, lane)
        back = Back(rows_ref, strip_ref, row, lane)
        cg, rden, _ = pointwise(
            field.strip_steps(), [full[6 + a, at, :] for a in range(3)], [full[a, at, :] for a in range(3)], full[WEIGHT, at, :]
        )
        rds[at, :] = rden
        tops[at, :] = cg[0]
        rs[at, :] = jnp.where(keep, jnp.where(lost, 0.0, back.strip(cg)), 0.0)
        for k in range(planes):
            cg, rden, wpart = pointwise(
                field.steps(k), [em[6 + a, k, at, :] for a in range(3)], [em[a, k, at, :] for a in range(3)], em[WEIGHT, k, at, :]
            )
            rd[k, at, :] = rden
            wp[k, at, :] = wpart
            r[k, at, :] = jnp.where(keep, back.plane(k, cg), 0.0)
            if k == planes - 1:
                top[at, :] = cg[0]

    plane_out(link, outs, [(top, tops)], [(r.at[0], rs)], planes, rows)


def second_step(counts, em, full, v, vs, *refs):
    planes, rows = em.shape[1], em.shape[2] - 2 * PAD
    nz = phases(counts["gz"])
    got_v, refs = refs[:nz], refs[nz:]
    (r1, r1s, rd, rds, wp, top1, top1s), refs = refs[:7], refs[7:]
    got_r, refs = refs[:nz], refs[nz:]
    (x, r2, r2s, top, tops, wg, dg), outs, scratch = refs[:7], refs[7 : 7 + nz], refs[7 + nz :]
    below, above, below_r, above_r, first, ghost, strip, first_r, ghost_r, strip_r, rows_ref, strip_ref = scratch
    link, row_link, col_link = (Link(a, counts[a]) for a in ("gz", "gx", "gy"))
    lane = lane_ids()
    part = lax.rem(lane, GROUP) // 4
    lost = jnp.logical_and(part == 1, jnp.logical_not(col_link.after))
    outside = jnp.logical_and(part == 2, jnp.logical_not(col_link.before))
    tiles, flat, folded = sizes(rows)
    plane_in(link, got_v, below, above)
    settle(
        v.at[1, 0], vs.at[1], em.at[3, planes - 1], full.at[3], below, above, flat + folded, link.after, first, ghost, strip, planes, rows
    )
    plane_in(link, got_r, below_r, above_r)
    settle(r1.at[0], r1s, top1, top1s, below_r, above_r, 0, link.after, first_r, ghost_r, strip_r, planes, rows)

    @pl.loop(0, tiles)
    def _(t):
        row = pl.multiple_of(SUB * t + SUB, SUB)
        at = pl.ds(row, SUB)
        keep = jnp.logical_or(t < tiles - 1, row_link.after)
        inside = jnp.logical_or(t > 0, row_link.before)
        field = Around(chooser(v.at[1], first, ghost, planes), strip, planes, row, lane)
        spread = Around(chooser(r1, first_r, ghost_r, planes), strip_r, planes, row, lane)
        back = Back(rows_ref, strip_ref, row, lane)

        rden = rds[at, :]
        down = spread.strip_steps()
        c = [jnp.where(inside, jnp.where(outside, 0.0, full[6 + a, at, :] * rden + down[a]), 0.0) for a in range(3)]
        cg, _, _ = pointwise(field.strip_steps(), c, [full[3 + a, at, :] for a in range(3)], full[WEIGHT, at, :])
        tops[at, :] = cg[0]
        r2s[at, :] = jnp.where(keep, jnp.where(lost, 0.0, back.strip(cg)), 0.0)
        for k in range(planes):
            rden = rd[k, at, :]
            down = spread.steps(k)
            c = [jnp.where(inside, em[6 + a, k, at, :] * rden + down[a], 0.0) for a in range(3)]
            cg, rden, wpart = pointwise(field.steps(k), c, [em[3 + a, k, at, :] for a in range(3)], em[WEIGHT, k, at, :])
            for a in range(3):
                x[a, k, at, :] = c[a] * rden
            wg[k, at, :] = wp[k, at, :] + wpart
            dg[k, at, :] = spread.now[k]
            r2[k, at, :] = jnp.where(keep, back.plane(k, cg), 0.0)
            if k == planes - 1:
                top[at, :] = cg[0]

    plane_out(link, outs, [(top, tops)], [(r2.at[0], r2s)], planes, rows)


def finish(counts, x, r2, r2s, top, tops, wg, dg, *refs):
    planes, rows = r2.shape[0], r2.shape[1] - 2 * PAD
    nz = phases(counts["gz"])
    got, (grad, weight_grad, data_grad), scratch = refs[:nz], refs[nz : nz + 3], refs[nz + 3 :]
    below, above, first, ghost, strip = scratch
    link = Link("gz", counts["gz"])
    lane = lane_ids()
    plane_in(link, got, below, above)
    settle(r2.at[0], r2s, top, tops, below, above, 0, link.after, first, ghost, strip, planes, rows)

    @pl.loop(0, rows // SUB)
    def _(t):
        row = pl.multiple_of(SUB * t + PAD, SUB)
        at, to = pl.ds(row, SUB), pl.ds(pl.multiple_of(SUB * t, SUB), SUB)
        spread = Around(chooser(r2, first, ghost, planes), strip, planes, row, lane)
        for k in range(planes):
            down = spread.steps(k)
            for a in range(3):
                grad[a, k, to, :] = x[a, k, at, :] + down[a]
            weight_grad[k, to, :] = wg[k, at, :]
            data_grad[k, to, :] = INVERSE * (dg[k, at, :] + spread.now[k])


def call(body, counts, operands, outs, scratch=()):
    held = pl.BlockSpec(memory_space=pltpu.VMEM)
    return pl.pallas_call(
        functools.partial(body, counts),
        out_shape=outs,
        in_specs=[held] * len(operands),
        out_specs=[held] * len(outs),
        scratch_shapes=list(scratch),
        compiler_params=pltpu.CompilerParams(vmem_limit_bytes=16 * 1024 * 1024),
        name=body.__name__,
    )(*operands)


def vmem(*shape):
    return pltpu.VMEM(shape, jnp.float32)


def shards(counts, data, weight, dual_start, dual_mid, cotangent):
    planes, rows, cols = data.shape
    held = rows + 2 * PAD
    tiles, flat, folded = sizes(rows)
    nx, ny, nz = (phases(counts[a]) for a in ("gx", "gy", "gz"))
    raw = (dual_mid, dual_start, cotangent, weight, data)
    block, strip, line = vmem(planes, held, cols), vmem(held, LANES), vmem(held, cols)

    sent = call(rows_out, counts, raw, [vmem(planes * offsets()[1], cols)] * nx)
    got = swap(sent, "gx", counts["gx"], "gy", counts["gy"])
    em, es, *sent = call(
        build, counts, (*raw, *got), [vmem(FIELDS, planes, held, cols), vmem(FIELDS, held, LANES)] + [vmem(2, flat, LANES)] * ny
    )
    got = swap(sent, "gy", counts["gy"], "gx", counts["gx"])
    one = flat + folded
    full, v, vs, *sent = call(
        strips_and_values,
        counts,
        (em, es, *got),
        [vmem(FIELDS, held, LANES), vmem(2, planes, held, cols), vmem(2, held, LANES)] + [vmem(2 * one, LANES)] * nz,
    )
    got_v = swap(sent, "gz", counts["gz"], "gy", counts["gy"])
    state = [block, strip, block, strip, block, line, strip]
    work = [line, line, strip]
    *first, = call(
        first_step,
        counts,
        (em, full, v, vs, *got_v),
        state + [vmem(one, LANES)] * nz,
        [vmem(2 * one, LANES)] * 2 + work + [block, strip],
    )
    got_r = swap(first[7:], "gz", counts["gz"], "gy", counts["gy"])
    *second, = call(
        second_step,
        counts,
        (em, full, v, vs, *got_v, *first[:7], *got_r),
        [vmem(3, planes, held, cols), block, strip, line, strip, block, block] + [vmem(one, LANES)] * nz,
        [vmem(2 * one, LANES)] * 2 + [vmem(one, LANES)] * 2 + work + work + [block, strip],
    )
    got = swap(second[7:], "gz", counts["gz"], "gy", counts["gy"])
    out = jax.ShapeDtypeStruct
    return tuple(call(
        finish,
        counts,
        (*second[:7], *got),
        [out(dual_mid.shape, jnp.float32), out(data.shape, jnp.float32), out(data.shape, jnp.float32)],
        [vmem(one, LANES)] * 2 + work,
    ))


def solution(mesh):
    field, dual = P("gz", "gx", "gy"), P(None, "gz", "gx", "gy")
    return jax.shard_map(
        functools.partial(shards, dict(mesh.shape)),
        mesh=mesh,
        in_specs=(field, field, dual, dual, dual),
        out_specs=(dual, field, field),
        check_vma=False,
    )
```

time: 142 us -> 79.4 us (0.56)
  starting transfers between devices: 46.7 us -> 0 us
  waiting for transfers between devices: 43.5 us -> 0 us
  blocking collectives: 0 us -> 37.9 us
  Pallas kernels: 0 us -> 34.6 us
  other arithmetic: 25.6 us -> 0 us
  local copies, waits for them, and re-layouts: 24.2 us -> 5.29 us
    ppermute x18 -> x0, starting transfers between devices: 46.7 us -> none  [the longest x9 32.8 us: extended(): lax.ppermute(tail, axis, [(i, (i + 1) % count) for i in range(ends)])]
    ppermute x18 -> x0, waiting for transfers between devices: 43.5 us -> none  [the longest x9 30.8 us: extended(): lax.ppermute(head, axis, [((i + 1) % count, i) for i in range(ends)])]
    all_gather x0 -> x9, blocking collectives: none -> 37.9 us  [the longest x4 19.4 us: swap(): lax.all_gather(values[1], (axis, spare), axis_index_groups=groups)]
    pallas_call x0 -> x6, Pallas kernels: none -> 34.6 us  [call(): pl.pallas_call(functools.partial(body, counts), out_shape=outs, in_specs=...]
    slice x13 -> x0, local copies, waits for them, and re-layouts: 13.1 us -> none  [the longest x9 8.55 us: extended(): lax.slice_in_dim(cells, cells.shape[dim] - width, cells.shape[dim], axis=...]
    concatenate x6 -> x0, other arithmetic: 11.1 us -> none  [extended(): jnp.concatenate([lax.ppermute(tail, axis, [(i, (i + 1) % count) for i in...]
    ppermute x8 -> x0, local copies, waits for them, and re-layouts: 8 us -> none  [the longest x4 4.65 us: extended(): lax.ppermute(head, axis, [((i + 1) % count, i) for i in range(ends)])]
    mul x4 -> x0, other arithmetic: 4.4 us -> none  [the longest x1 2.2 us: shards(): keeper * (divergence(padded[3:6], outer_ext) - scaled)]
  transfers between devices with their start and end apart: 18 -> 0, of which waited for: 12 -> 0; matrix products, arithmetic and copies ran while one was open for 6% -> 0% of each run, Pallas kernels for 0% -> 0%
where the time goes in v1:
time: 79.4 us; the launch traced here: 78.5 us
  blocking collectives  37.9 us (48%)
  Pallas kernels  34.6 us (44%)
  local copies, waits for them, and re-layouts  5.29 us (7%)
    pallas_call x6, Pallas kernels, call(): pl.pallas_call(functools.partial(body, counts), out_shape=outs, in_specs=...  34.6 us
    all_gather x4, blocking collectives, swap(): lax.all_gather(values[1], (axis, spare), axis_index_groups=groups)  19.4 us
    all_gather x5, blocking collectives, swap(): lax.all_gather(values[0], axis, axis_index_groups=[[i, i + 1] for i in ra...  18.6 us
    unnamed x10, local copies, waits for them, and re-layouts  5.29 us

profile of v1, /device:TPU:1, one launch (start us, length us, event | category | flops | bytes accessed | tf_op | source)
XLA Modules:
  0.0 78.5 jit_solution(8766260029647134533)
XLA Ops:
  0.6 0.0 copy-start
  0.6 1.1 %copy-done = f32[3,4,128,128]{3,2,1,0:T(8,128)S(1)} copy-done((f32[3,4,128,128]{3,2,1,0:T(8,128)S(1)}, f32[3,4,128,128]{3,2,1,0:T(8,128)}, u32[]{:S(2)}) %copy-start) | copy-done | bytes 786456
  1.8 0.0 copy-start.1
  1.8 1.1 %copy-done.1 = f32[3,4,128,128]{3,2,1,0:T(8,128)S(1)} copy-done((f32[3,4,128,128]{3,2,1,0:T(8,128)S(1)}, f32[3,4,128,128]{3,2,1,0:T(8,128)}, u32[]{:S(2)}) %copy-start.1) | copy-done | bytes 786456
  2.9 0.0 copy-start.2
  2.9 1.1 %copy-done.2 = f32[3,4,128,128]{3,2,1,0:T(8,128)S(1)} copy-done((f32[3,4,128,128]{3,2,1,0:T(8,128)S(1)}, f32[3,4,128,128]{3,2,1,0:T(8,128)}, u32[]{:S(2)}) %copy-start.2) | copy-done | bytes 786456
  4.0 0.0 copy-start.3
  4.0 0.9 %copy-done.3 = f32[4,128,128]{2,1,0:T(8,128)S(1)} copy-done((f32[4,128,128]{2,1,0:T(8,128)S(1)}, f32[4,128,128]{2,1,0:T(8,128)}, u32[]{:S(2)}) %copy-start.3) | copy-done | bytes 262168
  5.0 0.0 copy-start.4
  5.0 0.9 %copy-done.4 = f32[4,128,128]{2,1,0:T(8,128)S(1)} copy-done((f32[4,128,128]{2,1,0:T(8,128)S(1)}, f32[4,128,128]{2,1,0:T(8,128)}, u32[]{:S(2)}) %copy-start.4) | copy-done | bytes 262168
  6.0 4.3 %all-gather = f32[208,128]{1,0:T(8,128)S(1)} all-gather(f32[104,128]{1,0:T(8,128)S(1)} %get-tuple-element.31), channel_id=2, replica_groups={{0,8},{16,24},{1,9},{17,25},{2,10},{18,26},{3,11},{19,27},{4,12},{20,28..., dimensions={0}, use_global_device_ids=true | all-gather | bytes 159744 | tf_op jit(solution)/shard_map/all_gather | solution.py:38
  10.3 3.6 %all-gather.1 = f32[208,128]{1,0:T(8,128)S(1)} all-gather(f32[104,128]{1,0:T(8,128)S(1)} %get-tuple-element.32), channel_id=3, replica_groups={{8,16},{12,20},{0,4},{24,28},{9,17},{13,21},{1,5},{25,29},{10,18},{14,2..., dimensions={0}, use_global_device_ids=true | all-gather | bytes 159744 | tf_op jit(solution)/shard_map/all_gather | solution.py:43
  13.9 4.5 %build.1 = (f32[11,4,160,128]{3,2,1,0:T(8,128)S(1)}, f32[11,160,128]{2,1,0:T(8,128)S(1)}, f32[2,144,128]{2,1,0:T(8,128)S(1)}) custom-call(f32[3,4,128,128]{3,2,1,0:T(8,128)S(1)} %copy-done, f32[3,4,128,128]{3,2,1,0:T(8,128)S(1)} %copy-done.1, f32[3,4,128,128]{3,2,1,0:T(8,128)S(1)} %copy-done.2, f32[4,128,128]{2,1,0:T(8,128)S(1)} %copy-done.3, ...), custom_call_target="tpu_custom_call" | custom-call | tf_op jit(solution)/shard_map/build/pallas_call | solution.py:522
  18.4 4.7 %all-gather.2 = f32[4,144,128]{2,1,0:T(8,128)S(1)} all-gather(f32[2,144,128]{2,1,0:T(8,128)S(1)} %get-tuple-element.35), channel_id=4, replica_groups={{0,4},{1,5},{2,6},{3,7},{8,12},{9,13},{10,14},{11,15},{16,20},{17,21},{..., dimensions={0}, use_global_device_ids=true | all-gather | bytes 442368 | tf_op jit(solution)/shard_map/all_gather | solution.py:38
  23.1 8.8 %strips_and_values.1 = (f32[11,160,128]{2,1,0:T(8,128)S(1)}, f32[2,4,160,128]{3,2,1,0:T(8,128)S(1)}, f32[2,160,128]{2,1,0:T(8,128)S(1)}, f32[336,128]{1,0:T(8,128)S(1)}, f32[336,128]{1,0:T(8,128)S(1)}) custom-call(f32[11,4,160,128]{3,2,1,0:T(8,128)S(1)} %get-tuple-element.33.em, f32[11,160,128]{2,1,0:T(8,128)S(1)} %get-tuple-element.34.es, ...), custom_call_target="tpu_custom_call" | custom-call | tf_op jit(solution)/shard_map/strips_and_values/pallas_call | solution.py:522
  31.9 5.5 %all-gather.3 = f32[672,128]{1,0:T(8,128)S(1)} all-gather(f32[336,128]{1,0:T(8,128)S(1)} %get-tuple-element.39), channel_id=5, replica_groups={{0,1},{2,3},{4,5},{6,7},{8,9},{10,11},{12,13},{14,15},{16,17},{18,19},{..., dimensions={0}, use_global_device_ids=true | all-gather | bytes 516096 | tf_op jit(solution)/shard_map/all_gather | solution.py:38
  37.4 6.0 %all-gather.4 = f32[672,128]{1,0:T(8,128)S(1)} all-gather(f32[336,128]{1,0:T(8,128)S(1)} %get-tuple-element.40), channel_id=6, replica_groups={{1,2},{5,6},{0,4},{3,7},{9,10},{13,14},{8,12},{11,15},{17,18},{21,22},{..., dimensions={0}, use_global_device_ids=true | all-gather | bytes 516096 | tf_op jit(solution)/shard_map/all_gather | solution.py:43
  43.4 7.9 %first_step.1 = (f32[4,160,128]{2,1,0:T(8,128)S(1)}, f32[160,128]{1,0:T(8,128)S(1)}, f32[4,160,128]{2,1,0:T(8,128)S(1)}, f32[160,128]{1,0:T(8,128)S(1)}, f32[4,1...) custom-call(f32[11,4,160,128]{3,2,1,0:T(8,128)S(1)} %get-tuple-eleme, ...), custom_call_target="tpu_custom_call" | custom-call | tf_op jit(solution)/shard_map/first_step/pallas_call | solution.py:522
  51.2 2.0 %all-gather.5 = f32[336,128]{1,0:T(8,128)S(1)} all-gather(f32[168,128]{1,0:T(8,128)S(1)} %get-tuple-element.48), channel_id=7, replica_groups={{0,1},{2,3},{4,5},{6,7},{8,9},{10,11},{12,13},{14,15},{16,17},{18,19},{..., dimensions={0}, use_global_device_ids=true | all-gather | bytes 258048 | tf_op jit(solution)/shard_map/all_gather | solution.py:38
  53.2 4.9 %all-gather.6 = f32[336,128]{1,0:T(8,128)S(1)} all-gather(f32[168,128]{1,0:T(8,128)S(1)} %get-tuple-element.49), channel_id=8, replica_groups={{1,2},{5,6},{0,4},{3,7},{9,10},{13,14},{8,12},{11,15},{17,18},{21,22},{..., dimensions={0}, use_global_device_ids=true | all-gather | bytes 258048 | tf_op jit(solution)/shard_map/all_gather | solution.py:43
  58.1 9.4 %second_step.1 = (f32[3,4,160,128]{3,2,1,0:T(8,128)S(1)}, f32[4,160,128]{2,1,0:T(8,128)S(1)}, f32[160,128]{1,0:T(8,128)S(1)}, f32[160,128]{1,0:T(8,128)S(1)}, f3...) custom-call(f32[11,4,160,128]{3,2,1,0:T(8,128)S(1)} %get-tuple-eleme, ...), custom_call_target="tpu_custom_call" | custom-call | tf_op jit(solution)/shard_map/second_step/pallas_call | solution.py:522
  67.5 2.1 %all-gather.7 = f32[336,128]{1,0:T(8,128)S(1)} all-gather(f32[168,128]{1,0:T(8,128)S(1)} %get-tuple-element.57), channel_id=9, replica_groups={{0,1},{2,3},{4,5},{6,7},{8,9},{10,11},{12,13},{14,15},{16,17},{18,19},{..., dimensions={0}, use_global_device_ids=true | all-gather | bytes 258048 | tf_op jit(solution)/shard_map/all_gather | solution.py:38
  69.7 4.9 %all-gather.8 = f32[336,128]{1,0:T(8,128)S(1)} all-gather(f32[168,128]{1,0:T(8,128)S(1)} %get-tuple-element.58), channel_id=10, replica_groups={{1,2},{5,6},{0,4},{3,7},{9,10},{13,14},{8,12},{11,15},{17,18},{21,22},{..., dimensions={0}, use_global_device_ids=true | all-gather | bytes 258048 | tf_op jit(solution)/shard_map/all_gather | solution.py:43
  74.5 3.9 %finish.1 = (f32[3,4,128,128]{3,2,1,0:T(8,128)}, f32[4,128,128]{2,1,0:T(8,128)}, f32[4,128,128]{2,1,0:T(8,128)}) custom-call(f32[3,4,160,128]{3,2,1,0:T(8,128)S(1)} %get-tuple-element.50.x, f32[4,160,128]{2,1,0:T(8,128)S(1)} %get-tuple-element.51.r2, f32[160,128]{1,0:T(8,128)S(1)} %get-tuple-element.52.r2s, f32[160,128]{1,0:T(8,128)S(1)} %get-tuple-element.53.top, ...), custom_call_target="tpu_custom_call" | custom-call | tf_op jit(solution)/shard_map/finish/pallas_call | solution.py:522
  (1 shorter events, 0.0 us)
Async XLA Ops:
  0.6 1.1 %copy-start = (f32[3,4,128,128]{3,2,1,0:T(8,128)S(1)}, f32[3,4,128,128]{3,2,1,0:T(8,128)}, u32[]{:S(2)}) copy-start(f32[3,4,128,128]{3,2,1,0:T(8,128)} %dm.3) | copy-start | bytes 2359300
  1.8 1.1 %copy-start.1 = (f32[3,4,128,128]{3,2,1,0:T(8,128)S(1)}, f32[3,4,128,128]{3,2,1,0:T(8,128)}, u32[]{:S(2)}) copy-start(f32[3,4,128,128]{3,2,1,0:T(8,128)} %ds.3) | copy-start | bytes 2359300
  2.9 1.1 %copy-start.2 = (f32[3,4,128,128]{3,2,1,0:T(8,128)S(1)}, f32[3,4,128,128]{3,2,1,0:T(8,128)}, u32[]{:S(2)}) copy-start(f32[3,4,128,128]{3,2,1,0:T(8,128)} %ct.3) | copy-start | bytes 2359300
  4.0 0.9 %copy-start.3 = (f32[4,128,128]{2,1,0:T(8,128)S(1)}, f32[4,128,128]{2,1,0:T(8,128)}, u32[]{:S(2)}) copy-start(f32[4,128,128]{2,1,0:T(8,128)} %w.3) | copy-start | bytes 786436
  5.0 0.9 %copy-start.4 = (f32[4,128,128]{2,1,0:T(8,128)S(1)}, f32[4,128,128]{2,1,0:T(8,128)}, u32[]{:S(2)}) copy-start(f32[4,128,128]{2,1,0:T(8,128)} %d.3) | copy-start | bytes 786436

commit v2 on v1

--- a/solution.py
+++ b/solution.py
@@ -17,6 +17,7 @@
 WEIGHT, DATA = 9, 10
 PAD = 16
 SUB = 8
+UNROLL = 3
 LANES = 128
 GROUP = 16
 
@@ -68,6 +69,25 @@
     pl.when(jnp.logical_not(link.after))(lambda: after(None))
 
 
+class Later:
+    def __init__(self):
+        self.items = []
+
+    def put(self, ref, index, value):
+        self.items.append((ref, index, value))
+
+    def flush(self):
+        for ref, index, value in self.items:
+            ref[index] = value
+
+
+ALL = slice(None)
+
+
+def batches(count, size):
+    return [range(i, min(i + size, count)) for i in range(0, count, size)]
+
+
 def lane_ids():
     return lax.broadcasted_iota(jnp.int32, (SUB, LANES), 1)
 
@@ -101,23 +121,34 @@
     return out, total
 
 
-def rows_out(counts, dm, ds, ct, w, d, *outs):
-    planes, rows = d.shape[0], d.shape[1]
-    src = sources(dm, ds, ct, w, d)
+def rows_out(counts, *refs):
+    nx = phases(counts["gx"])
+    raw, outs, (*edges, sems) = refs[:5], refs[5 : 5 + nx], refs[5 + nx :]
+    planes, rows = raw[4].shape[0], raw[4].shape[1]
+    copies = []
+    for i, ref in enumerate(raw):
+        for end, at in enumerate((0, rows - SUB)):
+            rows_at = pl.ds(at, SUB)
+            view = ref.at[:, :, rows_at, :] if len(ref.shape) == 4 else ref.at[:, rows_at, :]
+            copies.append(pltpu.make_async_copy(view, edges[2 * i + end], sems.at[2 * i + end]))
+    for copy in copies:
+        copy.start()
+    for copy in copies:
+        copy.wait()
+    head, tail = sources(*edges[0::2]), sources(*edges[1::2])
     offs, per = offsets()
-    link = Link("gx", counts["gx"])
 
     def up(out):
         for f in range(FIELDS):
             for k in range(planes):
-                out[pl.ds(per * k + offs[f], BEFORE[f]), :] = src_rows(src[f], k, pl.ds(rows - BEFORE[f], BEFORE[f]))
+                out[pl.ds(per * k + offs[f], BEFORE[f]), :] = src_rows(tail[f], k, pl.ds(SUB - BEFORE[f], BEFORE[f]))
 
     def down(out):
         for f in range(FIELDS):
             for k in range(planes):
-                out[pl.ds(per * k + offs[f], AFTER[f]), :] = src_rows(src[f], k, pl.ds(0, AFTER[f]))
-
-    send(link, outs, up, down)
+                out[pl.ds(per * k + offs[f], AFTER[f]), :] = src_rows(head[f], k, pl.ds(0, AFTER[f]))
+
+    send(Link("gx", counts["gx"]), outs, up, down)
 
 
 def slot(f):
@@ -158,6 +189,7 @@
 
     def tile(row, read):
         packed = [[None, None] for _ in range(ny)]
+        later = Later()
         for f in range(FIELDS):
             strip = jnp.full((SUB, LANES), 1.0 if f == WEIGHT else 0.0, jnp.float32)
             for k in range(planes):
@@ -166,7 +198,7 @@
                 here = plane_of == k + 1
                 strip = jnp.where(jnp.logical_and(here, part == 0), turn(x, base + 4), strip)
                 strip = jnp.where(jnp.logical_and(here, part == 3), turn(x, base + 12), strip)
-            es[f, pl.ds(row, SUB), :] = strip
+            later.put(es, (f, pl.ds(row, SUB), ALL), strip)
             which, shift = slot(f)
             mask = jnp.logical_and(part == (f % 4), lane // 64 == (f // 4) % 2)
             for p in range(ny):
@@ -176,7 +208,8 @@
                 packed[p][which] = moved if old is None else jnp.where(mask, moved, old)
         for p in range(ny):
             for which in range(2):
-                outs[p][which, pl.ds(row - SUB, SUB), :] = packed[p][which]
+                later.put(outs[p], (which, pl.ds(row - SUB, SUB), ALL), packed[p][which])
+        later.flush()
 
     @pl.loop(0, rows // SUB)
     def _(t):
@@ -197,21 +230,21 @@
 
 
 def fold(strip, group, out, base, tiles):
-    lane = lane_ids()
+    group_of = lane_ids() // GROUP
     many = LANES // GROUP
-
-    @pl.loop(0, tiles)
-    def _(t):
-        side = lax.rem(t, many)
-        at = pl.ds(pl.multiple_of(base + SUB * (t // many), SUB), SUB)
-        x = strip[pl.ds(pl.multiple_of(SUB * t + SUB, SUB), SUB), :]
-        out[at, :] = jnp.where(lane // GROUP == side, turn(x, GROUP * (side - group)), out[at, :])
-
-
-def unfold(ref, base, t, group):
+    later = Later()
+    for i, some in enumerate(batches(tiles, many)):
+        x = None
+        for t in some:
+            y = turn(strip[pl.ds(SUB * t + SUB, SUB), :], GROUP * (t % many - group))
+            x = y if x is None else jnp.where(group_of == t % many, y, x)
+        later.put(out, (pl.ds(base + SUB * i, SUB), ALL), x)
+    later.flush()
+
+
+def unfold(read, base, t, group):
     many = LANES // GROUP
-    x = ref[pl.ds(pl.multiple_of(base + SUB * (t // many), SUB), SUB), :]
-    return turn(x, GROUP * (group - lax.rem(t, many)))
+    return turn(read(base + SUB * (t // many)), GROUP * (group - t % many))
 
 
 def sizes(rows):
@@ -221,9 +254,11 @@
 
 
 def copy_rows(src, out, base, tiles):
-    @pl.loop(0, tiles)
-    def _(t):
-        out[pl.ds(pl.multiple_of(base + SUB * t, SUB), SUB), :] = src[pl.ds(pl.multiple_of(SUB * t + SUB, SUB), SUB), :]
+    for some in batches(tiles, 9):
+        later = Later()
+        for t in some:
+            later.put(out, (pl.ds(base + SUB * t, SUB), ALL), src[pl.ds(SUB * t + SUB, SUB), :])
+        later.flush()
 
 
 def plane_out(link, outs, up, down, planes, rows):
@@ -241,17 +276,17 @@
     send(link, outs, put(up, planes), put(down, 1))
 
 
-def plane_in(link, ins, below, above):
-    def put(dst):
-        def fill(ref):
-            @pl.loop(0, dst.shape[0] // SUB)
-            def _(t):
-                at = pl.ds(pl.multiple_of(t * SUB, SUB), SUB)
-                dst[at, :] = jnp.zeros((SUB, LANES), jnp.float32) if ref is None else ref[at, :]
-
-        return fill
-
-    receive(link, ins, put(below), put(above))
+def plane_in(link, ins):
+    def at(index, first, known):
+        def read(row):
+            x = ins[0][index, pl.ds(row, SUB), :]
+            if len(ins) > 1:
+                x = jnp.where(first, x, ins[1][index, pl.ds(row, SUB), :])
+            return jnp.where(known, x, 0.0)
+
+        return read
+
+    return at(0, link.odd, link.before), at(1, link.even, link.after)
 
 
 def strips_and_values(counts, em, es, *refs):
@@ -269,8 +304,7 @@
     inner = lane // GROUP >= 2
     tiles, flat, folded = sizes(rows)
 
-    @pl.loop(0, tiles)
-    def _(t):
+    def strips(t, later):
         row = pl.multiple_of(SUB * t + SUB, SUB)
         at = pl.ds(pl.multiple_of(SUB * t, SUB), SUB)
 
@@ -286,10 +320,9 @@
             x = jnp.where(near, 1.0 if f == WEIGHT else 0.0, es[f, pl.ds(row, SUB), :])
             x = jnp.where(real_after, turn(blocks[1][which], GROUP + 4 - shift), x)
             x = jnp.where(real_before, turn(blocks[0][which], GROUP + 8 - shift), x)
-            full[f, pl.ds(row, SUB), :] = x
-
-    @pl.loop(0, tiles)
-    def _(t):
+            later.put(full, (f, pl.ds(row, SUB), ALL), x)
+
+    def values(t, later):
         row = pl.multiple_of(SUB * t + SUB, SUB)
         at, lower = pl.ds(row, SUB), pl.ds(row - 1, SUB)
         keep = jnp.logical_or(t < tiles - 1, row_link.after)
@@ -300,7 +333,7 @@
             x = x + (full[p1, at, :] - full[p1, lower, :])
             x = x + (s2 - turn(s2, 1))
             x = x - INVERSE * full[DATA, at, :]
-            vs[m, at, :] = jnp.where(keep, jnp.where(lost, 0.0, x), 0.0)
+            later.put(vs, (m, at, ALL), jnp.where(keep, jnp.where(lost, 0.0, x), 0.0))
             last = None
             for k in range(planes):
                 x = now = em[p0, k, at, :]
@@ -311,7 +344,16 @@
                 y = em[p2, k, at, :]
                 x = x + (y - col_before(y, s2, k, lane))
                 x = x - INVERSE * em[DATA, k, at, :]
-                v[m, k, at, :] = jnp.where(keep, x, 0.0)
+                later.put(v, (m, k, at, ALL), jnp.where(keep, x, 0.0))
+
+    for body in (strips, values):
+
+        @pl.loop(0, tiles // UNROLL)
+        def _(t):
+            later = Later()
+            for u in range(UNROLL):
+                body(t * UNROLL + u, later)
+            later.flush()
 
     plane_out(
         Link("gz", counts["gz"]),
@@ -325,20 +367,20 @@
 
 def settle(first, strip, last, last_strip, below, above, base, has_after, out_first, out_ghost, out_strip, planes, rows):
     tiles, flat, folded = sizes(rows)
-    lane = lane_ids()
-    group = lane // GROUP
-
-    @pl.loop(0, tiles)
-    def _(t):
-        at = pl.ds(pl.multiple_of(SUB * t + SUB, SUB), SUB)
-        sent = pl.ds(pl.multiple_of(base + SUB * t, SUB), SUB)
-        out_first[at, :] = first[at, :] - below[sent, :]
-        out_ghost[at, :] = jnp.where(has_after, above[sent, :] - last[at, :], 0.0)
-        x = strip[at, :]
-        x = jnp.where(group == 1, x - unfold(below, base + flat, t, 1), x)
-        ghost = unfold(above, base + flat, t, planes + 1) - turn(last_strip[at, :], GROUP)
-        ghost = jnp.where(has_after, ghost, 0.0)
-        out_strip[at, :] = jnp.where(group == planes + 1, ghost, x)
+    group = lane_ids() // GROUP
+    for some in batches(tiles, 6):
+        later = Later()
+        for t in some:
+            at = (pl.ds(SUB * t + SUB, SUB), ALL)
+            sent = base + SUB * t
+            later.put(out_first, at, first[at] - below(sent))
+            later.put(out_ghost, at, jnp.where(has_after, above(sent) - last[at], 0.0))
+            x = strip[at]
+            x = jnp.where(group == 1, x - unfold(below, base + flat, t, 1), x)
+            ghost = unfold(above, base + flat, t, planes + 1) - turn(last_strip[at], GROUP)
+            ghost = jnp.where(has_after, ghost, 0.0)
+            later.put(out_strip, at, jnp.where(group == planes + 1, ghost, x))
+        later.flush()
 
 
 def pointwise(g, c, p, w):
@@ -378,24 +420,38 @@
 
 
 class Back:
-    def __init__(self, rows_ref, strip_ref, row, lane):
-        self.rows_ref, self.strip_ref, self.lane = rows_ref, strip_ref, lane
-        self.at, self.lower = pl.ds(row, SUB), pl.ds(row - 1, SUB)
-        self.last = None
+    def __init__(self, carried, lane):
+        self.carried, self.lane = carried, lane
+        self.top = lax.broadcasted_iota(jnp.int32, (SUB, LANES), 0) == 0
+        self.last, self.out = None, []
+
+    def row_before(self, x):
+        down = pltpu.roll(x, 1, 0)
+        before = jnp.where(self.top, self.carried[len(self.out)], down)
+        self.out.append(down)
+        return before
 
     def strip(self, cg):
         self.s = cg[2]
-        self.strip_ref[self.at, :] = cg[1]
         x = cg[0] - jnp.where(self.lane // GROUP >= 2, turn(cg[0], GROUP), 0.0)
-        x = x + (cg[1] - self.strip_ref[self.lower, :])
+        x = x + (cg[1] - self.row_before(cg[1]))
         return x + (cg[2] - turn(cg[2], 1))
 
     def plane(self, k, cg):
-        self.rows_ref[k, self.at, :] = cg[1]
         x = cg[0] if self.last is None else cg[0] - self.last
         self.last = cg[0]
-        x = x + (cg[1] - self.rows_ref[k, self.lower, :])
+        x = x + (cg[1] - self.row_before(cg[1]))
         return x + (cg[2] - col_before(cg[2], self.s, k, self.lane))
+
+
+def over_tiles(tiles, planes, step):
+    def body(t, carried):
+        later = Later()
+        carried = step(t, carried, later)
+        later.flush()
+        return tuple(carried)
+
+    lax.fori_loop(0, tiles, body, (jnp.zeros((SUB, LANES), jnp.float32),) * (planes + 1))
 
 
 def chooser(mid, first, ghost, planes):
@@ -407,37 +463,38 @@
     nz = phases(counts["gz"])
     got, refs = refs[:nz], refs[nz:]
     (r, rs, rd, rds, wp, top, tops), outs, scratch = refs[:7], refs[7 : 7 + nz], refs[7 + nz :]
-    below, above, first, ghost, strip, rows_ref, strip_ref = scratch
+    first, ghost, strip = scratch
     link, row_link, col_link = (Link(a, counts[a]) for a in ("gz", "gx", "gy"))
     lane = lane_ids()
     lost = jnp.logical_and(lax.rem(lane, GROUP) // 4 == 1, jnp.logical_not(col_link.after))
     tiles, flat, folded = sizes(rows)
-    plane_in(link, got, below, above)
+    below, above = plane_in(link, got)
     settle(v.at[0, 0], vs.at[0], em.at[0, planes - 1], full.at[0], below, above, 0, link.after, first, ghost, strip, planes, rows)
 
-    @pl.loop(0, tiles)
-    def _(t):
+    def step(t, carried, later):
         row = pl.multiple_of(SUB * t + SUB, SUB)
         at = pl.ds(row, SUB)
         keep = jnp.logical_or(t < tiles - 1, row_link.after)
         field = Around(chooser(v.at[0], first, ghost, planes), strip, planes, row, lane)
-        back = Back(rows_ref, strip_ref, row, lane)
+        back = Back(carried, lane)
         cg, rden, _ = pointwise(
             field.strip_steps(), [full[6 + a, at, :] for a in range(3)], [full[a, at, :] for a in range(3)], full[WEIGHT, at, :]
         )
-        rds[at, :] = rden
-        tops[at, :] = cg[0]
-        rs[at, :] = jnp.where(keep, jnp.where(lost, 0.0, back.strip(cg)), 0.0)
+        later.put(rds, (at, ALL), rden)
+        later.put(tops, (at, ALL), cg[0])
+        later.put(rs, (at, ALL), jnp.where(keep, jnp.where(lost, 0.0, back.strip(cg)), 0.0))
         for k in range(planes):
             cg, rden, wpart = pointwise(
                 field.steps(k), [em[6 + a, k, at, :] for a in range(3)], [em[a, k, at, :] for a in range(3)], em[WEIGHT, k, at, :]
             )
-            rd[k, at, :] = rden
-            wp[k, at, :] = wpart
-            r[k, at, :] = jnp.where(keep, back.plane(k, cg), 0.0)
+            later.put(rd, (k, at, ALL), rden)
+            later.put(wp, (k, at, ALL), wpart)
+            later.put(r, (k, at, ALL), jnp.where(keep, back.plane(k, cg), 0.0))
             if k == planes - 1:
-                top[at, :] = cg[0]
-
+                later.put(top, (at, ALL), cg[0])
+        return back.out
+
+    over_tiles(tiles, planes, step)
     plane_out(link, outs, [(top, tops)], [(r.at[0], rs)], planes, rows)
 
 
@@ -448,49 +505,49 @@
     (r1, r1s, rd, rds, wp, top1, top1s), refs = refs[:7], refs[7:]
     got_r, refs = refs[:nz], refs[nz:]
     (x, r2, r2s, top, tops, wg, dg), outs, scratch = refs[:7], refs[7 : 7 + nz], refs[7 + nz :]
-    below, above, below_r, above_r, first, ghost, strip, first_r, ghost_r, strip_r, rows_ref, strip_ref = scratch
+    first, ghost, strip, first_r, ghost_r, strip_r = scratch
     link, row_link, col_link = (Link(a, counts[a]) for a in ("gz", "gx", "gy"))
     lane = lane_ids()
     part = lax.rem(lane, GROUP) // 4
     lost = jnp.logical_and(part == 1, jnp.logical_not(col_link.after))
     outside = jnp.logical_and(part == 2, jnp.logical_not(col_link.before))
     tiles, flat, folded = sizes(rows)
-    plane_in(link, got_v, below, above)
+    below, above = plane_in(link, got_v)
     settle(
         v.at[1, 0], vs.at[1], em.at[3, planes - 1], full.at[3], below, above, flat + folded, link.after, first, ghost, strip, planes, rows
     )
-    plane_in(link, got_r, below_r, above_r)
+    below_r, above_r = plane_in(link, got_r)
     settle(r1.at[0], r1s, top1, top1s, below_r, above_r, 0, link.after, first_r, ghost_r, strip_r, planes, rows)
 
-    @pl.loop(0, tiles)
-    def _(t):
+    def step(t, carried, later):
         row = pl.multiple_of(SUB * t + SUB, SUB)
         at = pl.ds(row, SUB)
         keep = jnp.logical_or(t < tiles - 1, row_link.after)
         inside = jnp.logical_or(t > 0, row_link.before)
         field = Around(chooser(v.at[1], first, ghost, planes), strip, planes, row, lane)
         spread = Around(chooser(r1, first_r, ghost_r, planes), strip_r, planes, row, lane)
-        back = Back(rows_ref, strip_ref, row, lane)
-
+        back = Back(carried, lane)
         rden = rds[at, :]
         down = spread.strip_steps()
         c = [jnp.where(inside, jnp.where(outside, 0.0, full[6 + a, at, :] * rden + down[a]), 0.0) for a in range(3)]
         cg, _, _ = pointwise(field.strip_steps(), c, [full[3 + a, at, :] for a in range(3)], full[WEIGHT, at, :])
-        tops[at, :] = cg[0]
-        r2s[at, :] = jnp.where(keep, jnp.where(lost, 0.0, back.strip(cg)), 0.0)
+        later.put(tops, (at, ALL), cg[0])
+        later.put(r2s, (at, ALL), jnp.where(keep, jnp.where(lost, 0.0, back.strip(cg)), 0.0))
         for k in range(planes):
             rden = rd[k, at, :]
             down = spread.steps(k)
             c = [jnp.where(inside, em[6 + a, k, at, :] * rden + down[a], 0.0) for a in range(3)]
             cg, rden, wpart = pointwise(field.steps(k), c, [em[3 + a, k, at, :] for a in range(3)], em[WEIGHT, k, at, :])
             for a in range(3):
-                x[a, k, at, :] = c[a] * rden
-            wg[k, at, :] = wp[k, at, :] + wpart
-            dg[k, at, :] = spread.now[k]
-            r2[k, at, :] = jnp.where(keep, back.plane(k, cg), 0.0)
+                later.put(x, (a, k, at, ALL), c[a] * rden)
+            later.put(wg, (k, at, ALL), wp[k, at, :] + wpart)
+            later.put(dg, (k, at, ALL), spread.now[k])
+            later.put(r2, (k, at, ALL), jnp.where(keep, back.plane(k, cg), 0.0))
             if k == planes - 1:
-                top[at, :] = cg[0]
-
+                later.put(top, (at, ALL), cg[0])
+        return back.out
+
+    over_tiles(tiles, planes, step)
     plane_out(link, outs, [(top, tops)], [(r2.at[0], r2s)], planes, rows)
 
 
@@ -498,34 +555,36 @@
     planes, rows = r2.shape[0], r2.shape[1] - 2 * PAD
     nz = phases(counts["gz"])
     got, (grad, weight_grad, data_grad), scratch = refs[:nz], refs[nz : nz + 3], refs[nz + 3 :]
-    below, above, first, ghost, strip = scratch
+    first, ghost, strip = scratch
     link = Link("gz", counts["gz"])
     lane = lane_ids()
-    plane_in(link, got, below, above)
+    below, above = plane_in(link, got)
     settle(r2.at[0], r2s, top, tops, below, above, 0, link.after, first, ghost, strip, planes, rows)
 
-    @pl.loop(0, rows // SUB)
+    @pl.loop(0, rows // SUB, unroll=2)
     def _(t):
         row = pl.multiple_of(SUB * t + PAD, SUB)
         at, to = pl.ds(row, SUB), pl.ds(pl.multiple_of(SUB * t, SUB), SUB)
         spread = Around(chooser(r2, first, ghost, planes), strip, planes, row, lane)
+        later = Later()
         for k in range(planes):
             down = spread.steps(k)
             for a in range(3):
-                grad[a, k, to, :] = x[a, k, at, :] + down[a]
-            weight_grad[k, to, :] = wg[k, at, :]
-            data_grad[k, to, :] = INVERSE * (dg[k, at, :] + spread.now[k])
-
-
-def call(body, counts, operands, outs, scratch=()):
+                later.put(grad, (a, k, to, ALL), x[a, k, at, :] + down[a])
+            later.put(weight_grad, (k, to, ALL), wg[k, at, :])
+            later.put(data_grad, (k, to, ALL), INVERSE * (dg[k, at, :] + spread.now[k]))
+        later.flush()
+
+
+def call(body, counts, operands, outs, scratch=(), space=pltpu.VMEM, grant=16):
     held = pl.BlockSpec(memory_space=pltpu.VMEM)
     return pl.pallas_call(
         functools.partial(body, counts),
         out_shape=outs,
-        in_specs=[held] * len(operands),
+        in_specs=[pl.BlockSpec(memory_space=space)] * len(operands),
         out_specs=[held] * len(outs),
         scratch_shapes=list(scratch),
-        compiler_params=pltpu.CompilerParams(vmem_limit_bytes=16 * 1024 * 1024),
+        compiler_params=pltpu.CompilerParams(vmem_limit_bytes=grant * 1024 * 1024),
         name=body.__name__,
     )(*operands)
 
@@ -542,7 +601,15 @@
     raw = (dual_mid, dual_start, cotangent, weight, data)
     block, strip, line = vmem(planes, held, cols), vmem(held, LANES), vmem(held, cols)
 
-    sent = call(rows_out, counts, raw, [vmem(planes * offsets()[1], cols)] * nx)
+    sent = call(
+        rows_out,
+        counts,
+        raw,
+        [vmem(planes * offsets()[1], cols)] * nx,
+        [vmem(*x.shape[:-2], SUB, cols) for x in raw for _ in range(2)] + [pltpu.SemaphoreType.DMA((2 * len(raw),))],
+        pltpu.HBM,
+        60,
+    )
     got = swap(sent, "gx", counts["gx"], "gy", counts["gy"])
     em, es, *sent = call(
         build, counts, (*raw, *got), [vmem(FIELDS, planes, held, cols), vmem(FIELDS, held, LANES)] + [vmem(2, flat, LANES)] * ny
@@ -563,7 +630,7 @@
         counts,
         (em, full, v, vs, *got_v),
         state + [vmem(one, LANES)] * nz,
-        [vmem(2 * one, LANES)] * 2 + work + [block, strip],
+        work,
     )
     got_r = swap(first[7:], "gz", counts["gz"], "gy", counts["gy"])
     *second, = call(
@@ -571,7 +638,7 @@
         counts,
         (em, full, v, vs, *got_v, *first[:7], *got_r),
         [vmem(3, planes, held, cols), block, strip, line, strip, block, block] + [vmem(one, LANES)] * nz,
-        [vmem(2 * one, LANES)] * 2 + [vmem(one, LANES)] * 2 + work + work + [block, strip],
+        work + work,
     )
     got = swap(second[7:], "gz", counts["gz"], "gy", counts["gy"])
     out = jax.ShapeDtypeStruct
@@ -580,7 +647,7 @@
         counts,
         (*second[:7], *got),
         [out(dual_mid.shape, jnp.float32), out(data.shape, jnp.float32), out(data.shape, jnp.float32)],
-        [vmem(one, LANES)] * 2 + work,
+        work,
     ))
 
 

time: 79.4 us -> 57.9 us (0.73)
  Pallas kernels: 34.6 us -> 16.3 us
  local copies, waits for them, and re-layouts: 5.29 us -> 1.91 us
    pallas_call x6, Pallas kernels: 34.6 us -> 16.3 us  [call(): pl.pallas_call(functools.partial(body, counts), out_shape=outs, in_specs=...]
    unnamed x10, local copies, waits for them, and re-layouts: 5.29 us -> 1.91 us
where the time goes in v2:
time: 57.9 us; the launch traced here: 57 us
  blocking collectives  38.1 us (66%)
  Pallas kernels  16.3 us (28%)
  local copies, waits for them, and re-layouts  1.91 us (3%)
  between operations  0.71 us (1%)
    all_gather x4, blocking collectives, swap(): lax.all_gather(values[1], (axis, spare), axis_index_groups=groups)  19.4 us
    all_gather x5, blocking collectives, swap(): lax.all_gather(values[0], axis, axis_index_groups=[[i, i + 1] for i in ra...  18.7 us
    pallas_call x6, Pallas kernels, call(): pl.pallas_call(functools.partial(body, counts), out_shape=outs, in_specs=...  16.3 us
    unnamed x10, local copies, waits for them, and re-layouts  1.91 us

profile of v2, /device:TPU:1, one launch (start us, length us, event | category | flops | bytes accessed | tf_op | source)
XLA Modules:
  0.0 57.0 jit_solution(5474788999361121991)
XLA Ops:
  0.6 0.0 copy-start.2
  0.6 0.0 copy-start
  0.7 0.0 copy-start.1
  0.7 1.2 %rows_out.1 = (f32[104,128]{1,0:T(8,128)S(1)}, f32[104,128]{1,0:T(8,128)S(1)}) custom-call(f32[3,4,128,128]{3,2,1,0:T(8,128)} %dm.1, f32[3,4,128,128]{3,2,1,0:T(8,128)} %ds.1, f32[3,4,128,128]{3,2,1,0:T(8,128)} %ct.1, f32[4,128,128]{2,1,0:T(8,128)} %w.1, f32[4,128,128]{2,1,0:T(8,128)} %d.1), custom_call_target="tpu_custom_call" | custom-call | tf_op jit(solution)/shard_map/rows_out/pallas_call | solution.py:581
  1.9 4.3 %all-gather = f32[208,128]{1,0:T(8,128)S(1)} all-gather(f32[104,128]{1,0:T(8,128)S(1)} %get-tuple-element.31), channel_id=2, replica_groups={{0,8},{16,24},{1,9},{17,25},{2,10},{18,26},{3,11},{19,27},{4,12},{20,28..., dimensions={0}, use_global_device_ids=true | all-gather | bytes 159744 | tf_op jit(solution)/shard_map/all_gather | solution.py:39
  6.2 3.6 %all-gather.1 = f32[208,128]{1,0:T(8,128)S(1)} all-gather(f32[104,128]{1,0:T(8,128)S(1)} %get-tuple-element.32), channel_id=3, replica_groups={{8,16},{12,20},{0,4},{24,28},{9,17},{13,21},{1,5},{25,29},{10,18},{14,2..., dimensions={0}, use_global_device_ids=true | all-gather | bytes 159744 | tf_op jit(solution)/shard_map/all_gather | solution.py:44
  9.8 0.0 copy-done.2
  9.8 0.0 copy-done
  9.8 0.0 copy-done.1
  9.8 0.0 copy-start.3
  9.8 0.9 %copy-done.3 = f32[4,128,128]{2,1,0:T(8,128)S(1)} copy-done((f32[4,128,128]{2,1,0:T(8,128)S(1)}, f32[4,128,128]{2,1,0:T(8,128)}, u32[]{:S(2)}) %copy-start.3) | copy-done | bytes 262168
  10.8 0.0 copy-start.4
  10.8 0.9 %copy-done.4 = f32[4,128,128]{2,1,0:T(8,128)S(1)} copy-done((f32[4,128,128]{2,1,0:T(8,128)S(1)}, f32[4,128,128]{2,1,0:T(8,128)}, u32[]{:S(2)}) %copy-start.4) | copy-done | bytes 262168
  11.7 4.4 %build.1 = (f32[11,4,160,128]{3,2,1,0:T(8,128)S(1)}, f32[11,160,128]{2,1,0:T(8,128)S(1)}, f32[2,144,128]{2,1,0:T(8,128)S(1)}) custom-call(f32[3,4,128,128]{3,2,1,0:T(8,128)S(1)} %copy-done, f32[3,4,128,128]{3,2,1,0:T(8,128)S(1)} %copy-done.1, f32[3,4,128,128]{3,2,1,0:T(8,128)S(1)} %copy-done.2, f32[4,128,128]{2,1,0:T(8,128)S(1)} %copy-done.3, ...), custom_call_target="tpu_custom_call" | custom-call | tf_op jit(solution)/shard_map/build/pallas_call | solution.py:581
  16.1 4.7 %all-gather.2 = f32[4,144,128]{2,1,0:T(8,128)S(1)} all-gather(f32[2,144,128]{2,1,0:T(8,128)S(1)} %get-tuple-element.35), channel_id=4, replica_groups={{0,4},{1,5},{2,6},{3,7},{8,12},{9,13},{10,14},{11,15},{16,20},{17,21},{..., dimensions={0}, use_global_device_ids=true | all-gather | bytes 442368 | tf_op jit(solution)/shard_map/all_gather | solution.py:39
  20.8 1.8 %strips_and_values.1 = (f32[11,160,128]{2,1,0:T(8,128)S(1)}, f32[2,4,160,128]{3,2,1,0:T(8,128)S(1)}, f32[2,160,128]{2,1,0:T(8,128)S(1)}, f32[336,128]{1,0:T(8,128)S(1)}, f32[336,128]{1,0:T(8,128)S(1)}) custom-call(f32[11,4,160,128]{3,2,1,0:T(8,128)S(1)} %get-tuple-element.33.em, f32[11,160,128]{2,1,0:T(8,128)S(1)} %get-tuple-element.34.es, ...), custom_call_target="tpu_custom_call" | custom-call | tf_op jit(solution)/shard_map/strips_and_values/pallas_call | solution.py:581
  22.6 5.5 %all-gather.3 = f32[672,128]{1,0:T(8,128)S(1)} all-gather(f32[336,128]{1,0:T(8,128)S(1)} %get-tuple-element.39), channel_id=5, replica_groups={{0,1},{2,3},{4,5},{6,7},{8,9},{10,11},{12,13},{14,15},{16,17},{18,19},{..., dimensions={0}, use_global_device_ids=true | all-gather | bytes 516096 | tf_op jit(solution)/shard_map/all_gather | solution.py:39
  28.1 6.0 %all-gather.4 = f32[672,128]{1,0:T(8,128)S(1)} all-gather(f32[336,128]{1,0:T(8,128)S(1)} %get-tuple-element.40), channel_id=6, replica_groups={{1,2},{5,6},{0,4},{3,7},{9,10},{13,14},{8,12},{11,15},{17,18},{21,22},{..., dimensions={0}, use_global_device_ids=true | all-gather | bytes 516096 | tf_op jit(solution)/shard_map/all_gather | solution.py:44
  34.1 3.5 %first_step.1 = (f32[4,160,128]{2,1,0:T(8,128)S(1)}, f32[160,128]{1,0:T(8,128)S(1)}, f32[4,160,128]{2,1,0:T(8,128)S(1)}, f32[160,128]{1,0:T(8,128)S(1)}, f32[4,1...) custom-call(f32[11,4,160,128]{3,2,1,0:T(8,128)S(1)} %get-tuple-eleme, ...), custom_call_target="tpu_custom_call" | custom-call | tf_op jit(solution)/shard_map/first_step/pallas_call | solution.py:581
  37.6 2.0 %all-gather.5 = f32[336,128]{1,0:T(8,128)S(1)} all-gather(f32[168,128]{1,0:T(8,128)S(1)} %get-tuple-element.48), channel_id=7, replica_groups={{0,1},{2,3},{4,5},{6,7},{8,9},{10,11},{12,13},{14,15},{16,17},{18,19},{..., dimensions={0}, use_global_device_ids=true | all-gather | bytes 258048 | tf_op jit(solution)/shard_map/all_gather | solution.py:39
  39.6 4.9 %all-gather.6 = f32[336,128]{1,0:T(8,128)S(1)} all-gather(f32[168,128]{1,0:T(8,128)S(1)} %get-tuple-element.49), channel_id=8, replica_groups={{1,2},{5,6},{0,4},{3,7},{9,10},{13,14},{8,12},{11,15},{17,18},{21,22},{..., dimensions={0}, use_global_device_ids=true | all-gather | bytes 258048 | tf_op jit(solution)/shard_map/all_gather | solution.py:44
  44.5 3.6 %second_step.1 = (f32[3,4,160,128]{3,2,1,0:T(8,128)S(1)}, f32[4,160,128]{2,1,0:T(8,128)S(1)}, f32[160,128]{1,0:T(8,128)S(1)}, f32[160,128]{1,0:T(8,128)S(1)}, f3...) custom-call(f32[11,4,160,128]{3,2,1,0:T(8,128)S(1)} %get-tuple-eleme, ...), custom_call_target="tpu_custom_call" | custom-call | tf_op jit(solution)/shard_map/second_step/pallas_call | solution.py:581
  48.1 2.2 %all-gather.7 = f32[336,128]{1,0:T(8,128)S(1)} all-gather(f32[168,128]{1,0:T(8,128)S(1)} %get-tuple-element.57), channel_id=9, replica_groups={{0,1},{2,3},{4,5},{6,7},{8,9},{10,11},{12,13},{14,15},{16,17},{18,19},{..., dimensions={0}, use_global_device_ids=true | all-gather | bytes 258048 | tf_op jit(solution)/shard_map/all_gather | solution.py:39
  50.3 4.9 %all-gather.8 = f32[336,128]{1,0:T(8,128)S(1)} all-gather(f32[168,128]{1,0:T(8,128)S(1)} %get-tuple-element.58), channel_id=10, replica_groups={{1,2},{5,6},{0,4},{3,7},{9,10},{13,14},{8,12},{11,15},{17,18},{21,22},{..., dimensions={0}, use_global_device_ids=true | all-gather | bytes 258048 | tf_op jit(solution)/shard_map/all_gather | solution.py:44
  55.2 1.8 %finish.1 = (f32[3,4,128,128]{3,2,1,0:T(8,128)}, f32[4,128,128]{2,1,0:T(8,128)}, f32[4,128,128]{2,1,0:T(8,128)}) custom-call(f32[3,4,160,128]{3,2,1,0:T(8,128)S(1)} %get-tuple-element.50.x, f32[4,160,128]{2,1,0:T(8,128)S(1)} %get-tuple-element.51.r2, f32[160,128]{1,0:T(8,128)S(1)} %get-tuple-element.52.r2s, f32[160,128]{1,0:T(8,128)S(1)} %get-tuple-element.53.top, ...), custom_call_target="tpu_custom_call" | custom-call | tf_op jit(solution)/shard_map/finish/pallas_call | solution.py:581
Async XLA Ops:
  0.6 9.2 %copy-start.2 = (f32[3,4,128,128]{3,2,1,0:T(8,128)S(1)}, f32[3,4,128,128]{3,2,1,0:T(8,128)}, u32[]{:S(2)}) copy-start(f32[3,4,128,128]{3,2,1,0:T(8,128)} %ct.1) | copy-start | bytes 2359300
  0.6 9.2 %copy-start = (f32[3,4,128,128]{3,2,1,0:T(8,128)S(1)}, f32[3,4,128,128]{3,2,1,0:T(8,128)}, u32[]{:S(2)}) copy-start(f32[3,4,128,128]{3,2,1,0:T(8,128)} %dm.1) | copy-start | bytes 2359300
  0.7 9.2 %copy-start.1 = (f32[3,4,128,128]{3,2,1,0:T(8,128)S(1)}, f32[3,4,128,128]{3,2,1,0:T(8,128)}, u32[]{:S(2)}) copy-start(f32[3,4,128,128]{3,2,1,0:T(8,128)} %ds.1) | copy-start | bytes 2359300
  9.8 1.0 %copy-start.3 = (f32[4,128,128]{2,1,0:T(8,128)S(1)}, f32[4,128,128]{2,1,0:T(8,128)}, u32[]{:S(2)}) copy-start(f32[4,128,128]{2,1,0:T(8,128)} %w.1) | copy-start | bytes 786436
  10.8 0.9 %copy-start.4 = (f32[4,128,128]{2,1,0:T(8,128)S(1)}, f32[4,128,128]{2,1,0:T(8,128)}, u32[]{:S(2)}) copy-start(f32[4,128,128]{2,1,0:T(8,128)} %d.1) | copy-start | bytes 786436

commit v3 on v2

--- a/solution.py
+++ b/solution.py
@@ -18,6 +18,7 @@
 PAD = 16
 SUB = 8
 UNROLL = 3
+TOGETHER = 3
 LANES = 128
 GROUP = 16
 
@@ -96,6 +97,10 @@
     return pltpu.roll(x, by % LANES if isinstance(by, int) else lax.rem(by + 4 * LANES, LANES), 1)
 
 
+def take(x, lanes):
+    return jnp.take_along_axis(x, lanes, axis=1)
+
+
 def col_before(x, strip, k, lane):
     return jnp.where(lane == 0, turn(strip, -(GROUP * (k + 1) + 11)), turn(x, 1))
 
@@ -123,7 +128,7 @@
 
 def rows_out(counts, *refs):
     nx = phases(counts["gx"])
-    raw, outs, (*edges, sems) = refs[:5], refs[5 : 5 + nx], refs[5 + nx :]
+    raw, whole, outs, (*edges, sems) = refs[:5], refs[5:7], refs[7 : 7 + nx], refs[7 + nx :]
     planes, rows = raw[4].shape[0], raw[4].shape[1]
     copies = []
     for i, ref in enumerate(raw):
@@ -131,7 +136,8 @@
             rows_at = pl.ds(at, SUB)
             view = ref.at[:, :, rows_at, :] if len(ref.shape) == 4 else ref.at[:, rows_at, :]
             copies.append(pltpu.make_async_copy(view, edges[2 * i + end], sems.at[2 * i + end]))
-    for copy in copies:
+    late = [pltpu.make_async_copy(raw[3 + i], whole[i], sems.at[2 * len(raw) + i]) for i in range(2)]
+    for copy in copies + late:
         copy.start()
     for copy in copies:
         copy.wait()
@@ -149,10 +155,35 @@
                 out[pl.ds(per * k + offs[f], AFTER[f]), :] = src_rows(head[f], k, pl.ds(0, AFTER[f]))
 
     send(Link("gx", counts["gx"]), outs, up, down)
-
-
-def slot(f):
-    return f // 8, 4 * (f % 4) + 64 * ((f // 4) % 2)
+    for copy in late:
+        copy.wait()
+
+
+def column_lanes(planes):
+    firsts, total = [], 0
+    for f in range(FIELDS):
+        firsts.append(total)
+        total += planes * AFTER[f]
+    return firsts
+
+
+def pack_lanes(lane, planes, up):
+    out, firsts = jnp.zeros_like(lane), column_lanes(planes)
+    for f in range(FIELDS):
+        deep = AFTER[f]
+        for k in range(planes):
+            first = firsts[f] + k * deep
+            at = GROUP * (k + 1) + jnp.where(up, 4 - deep, 12)
+            out = jnp.where(lane >= first, lane - first + at, out)
+    return jnp.minimum(out, LANES - 1)
+
+
+def unpack_lanes(lane, planes, f):
+    deep = AFTER[f]
+    step = lax.rem(lane, 4)
+    step = jnp.where(lax.rem(lane, GROUP) // 4 == 1, step, step - (4 - deep))
+    plane = lane // GROUP - 1
+    return jnp.clip(column_lanes(planes)[f] + plane * deep + step, 0, LANES - 1)
 
 
 def build(counts, dm, ds, ct, w, d, *refs):
@@ -173,6 +204,7 @@
                     else:
                         at, many = start(counted[f]), counted[f]
                         value = ref[pl.ds(per * k + offs[f], many), :]
+                        value = 1.0 / value if f == WEIGHT else value
                     em[f, k, pl.ds(at, many), :] = value
 
         return fill
@@ -186,47 +218,45 @@
     link = Link("gy", counts["gy"])
     part = lax.rem(lane, GROUP) // 4
     plane_of = lane // GROUP
-
-    def tile(row, read):
-        packed = [[None, None] for _ in range(ny)]
-        later = Later()
+    own = jnp.logical_or(part == 0, part == 3)
+    edges = lax.rem(lane, 4) + jnp.where(part == 0, LANES - 4, 0)
+    packing = [pack_lanes(lane, planes, link.even if p == 0 else link.odd) for p in range(ny)]
+
+    def tile(row, read, later):
+        packed = [None] * ny
         for f in range(FIELDS):
             strip = jnp.full((SUB, LANES), 1.0 if f == WEIGHT else 0.0, jnp.float32)
             for k in range(planes):
-                x = read(f, k)
-                base = GROUP * (k + 1)
-                here = plane_of == k + 1
-                strip = jnp.where(jnp.logical_and(here, part == 0), turn(x, base + 4), strip)
-                strip = jnp.where(jnp.logical_and(here, part == 3), turn(x, base + 12), strip)
+                strip = jnp.where(jnp.logical_and(own, plane_of == k + 1), take(read(f, k), edges), strip)
             later.put(es, (f, pl.ds(row, SUB), ALL), strip)
-            which, shift = slot(f)
-            mask = jnp.logical_and(part == (f % 4), lane // 64 == (f // 4) % 2)
             for p in range(ny):
-                up = link.even if p == 0 else link.odd
-                moved = turn(strip, shift - GROUP + jnp.where(up, 0, -12))
-                old = packed[p][which]
-                packed[p][which] = moved if old is None else jnp.where(mask, moved, old)
+                moved = take(strip, packing[p])
+                packed[p] = moved if f == 0 else jnp.where(lane >= column_lanes(planes)[f], moved, packed[p])
         for p in range(ny):
-            for which in range(2):
-                later.put(outs[p], (which, pl.ds(row - SUB, SUB), ALL), packed[p][which])
-        later.flush()
+            later.put(outs[p], (pl.ds(row - SUB, SUB), ALL), packed[p])
 
     @pl.loop(0, rows // SUB)
     def _(t):
         inside = pl.multiple_of(t * SUB, SUB)
         row = pl.multiple_of(t * SUB + PAD, SUB)
 
+        later = Later()
+
         def read(f, k):
             x = src_rows(src[f], k, pl.ds(inside, SUB))
+            x = 1.0 / x if f == WEIGHT else x
             em[f, k, pl.ds(row, SUB), :] = x
             return x
 
-        tile(row, read)
+        tile(row, read, later)
+        later.flush()
 
     @pl.loop(0, 2)
     def _(t):
+        later = Later()
         row = pl.multiple_of(PAD - SUB + t * (rows + SUB), SUB)
-        tile(row, lambda f, k: em[f, k, pl.ds(row, SUB), :])
+        tile(row, lambda f, k: em[f, k, pl.ds(row, SUB), :], later)
+        later.flush()
 
 
 def fold(strip, group, out, base, tiles):
@@ -300,6 +330,15 @@
     near = jnp.logical_or(part == 1, part == 2)
     real_after = jnp.logical_and(part == 1, link.after)
     real_before = jnp.logical_and(part == 2, link.before)
+    lanes = [unpack_lanes(lane, planes, f) for f in range(FIELDS)]
+    if ny == 1:
+        other = jnp.where(link.even, 1, 0)
+        blocks = [(lambda at: got[0][other, at, :], jnp.logical_or(real_after, real_before))]
+    else:
+        blocks = [
+            (lambda at: jnp.where(link.even, got[0][1, at, :], got[1][1, at, :]), real_after),
+            (lambda at: jnp.where(link.odd, got[0][0, at, :], got[1][0, at, :]), real_before),
+        ]
     lost = jnp.logical_and(part == 1, jnp.logical_not(link.after))
     inner = lane // GROUP >= 2
     tiles, flat, folded = sizes(rows)
@@ -308,18 +347,10 @@
         row = pl.multiple_of(SUB * t + SUB, SUB)
         at = pl.ds(pl.multiple_of(SUB * t, SUB), SUB)
 
-        def sent(which, index):
-            if ny == 1:
-                return got[0][index, which, at, :]
-            first = link.odd if index == 0 else link.even
-            return jnp.where(first, got[0][index, which, at, :], got[1][index, which, at, :])
-
-        blocks = [[sent(which, index) for which in range(2)] for index in range(2)]
         for f in range(FIELDS):
-            which, shift = slot(f)
             x = jnp.where(near, 1.0 if f == WEIGHT else 0.0, es[f, pl.ds(row, SUB), :])
-            x = jnp.where(real_after, turn(blocks[1][which], GROUP + 4 - shift), x)
-            x = jnp.where(real_before, turn(blocks[0][which], GROUP + 8 - shift), x)
+            for block, mask in blocks:
+                x = jnp.where(mask, take(block(at), lanes[f]), x)
             later.put(full, (f, pl.ds(row, SUB), ALL), x)
 
     def values(t, later):
@@ -383,11 +414,10 @@
         later.flush()
 
 
-def pointwise(g, c, p, w):
+def pointwise(g, c, p, rw):
     q = g[0] * g[0] + g[1] * g[1] + g[2] * g[2] + SMOOTH
     rn = lax.rsqrt(q)
     tn = STEP * (q * rn)
-    rw = 1.0 / w
     rden = 1.0 / (1.0 + tn * rw)
     inner = c[0] * p[0] + c[1] * p[1] + c[2] * p[2]
     inner = inner + STEP * (c[0] * g[0] + c[1] * g[1] + c[2] * g[2])
@@ -447,11 +477,12 @@
 def over_tiles(tiles, planes, step):
     def body(t, carried):
         later = Later()
-        carried = step(t, carried, later)
+        for u in range(TOGETHER):
+            carried = step(t * TOGETHER + u, carried, later)
         later.flush()
         return tuple(carried)
 
-    lax.fori_loop(0, tiles, body, (jnp.zeros((SUB, LANES), jnp.float32),) * (planes + 1))
+    lax.fori_loop(0, tiles // TOGETHER, body, (jnp.zeros((SUB, LANES), jnp.float32),) * (planes + 1))
 
 
 def chooser(mid, first, ghost, planes):
@@ -601,18 +632,18 @@
     raw = (dual_mid, dual_start, cotangent, weight, data)
     block, strip, line = vmem(planes, held, cols), vmem(held, LANES), vmem(held, cols)
 
-    sent = call(
+    near_weight, near_data, *sent = call(
         rows_out,
         counts,
         raw,
-        [vmem(planes * offsets()[1], cols)] * nx,
-        [vmem(*x.shape[:-2], SUB, cols) for x in raw for _ in range(2)] + [pltpu.SemaphoreType.DMA((2 * len(raw),))],
+        [vmem(*data.shape)] * 2 + [vmem(planes * offsets()[1], cols)] * nx,
+        [vmem(*x.shape[:-2], SUB, cols) for x in raw for _ in range(2)] + [pltpu.SemaphoreType.DMA((2 * len(raw) + 2,))],
         pltpu.HBM,
         60,
     )
     got = swap(sent, "gx", counts["gx"], "gy", counts["gy"])
     em, es, *sent = call(
-        build, counts, (*raw, *got), [vmem(FIELDS, planes, held, cols), vmem(FIELDS, held, LANES)] + [vmem(2, flat, LANES)] * ny
+        build, counts, (*raw[:3], near_weight, near_data, *got), [vmem(FIELDS, planes, held, cols), vmem(FIELDS, held, LANES)] + [vmem(flat, LANES)] * ny
     )
     got = swap(sent, "gy", counts["gy"], "gx", counts["gx"])
     one = flat + folded

time: 57.9 us -> 51.1 us (0.88)
  Pallas kernels: 16.3 us -> 12.3 us
  local copies, waits for them, and re-layouts: 1.91 us -> 0.01 us
  blocking collectives: 38.1 us -> 37.3 us
    pallas_call x6, Pallas kernels: 16.3 us -> 12.3 us  [call(): pl.pallas_call(functools.partial(body, counts), out_shape=outs, in_specs=...]
    unnamed x10 -> x6, local copies, waits for them, and re-layouts: 1.91 us -> 0.01 us
    all_gather x5, blocking collectives: 18.7 us -> 17.9 us  [swap(): lax.all_gather(values[0], axis, axis_index_groups=[[i, i + 1] for i in ra...]
where the time goes in v3:
time: 51.1 us; the launch traced here: 50.3 us
  blocking collectives  37.3 us (73%)
  Pallas kernels  12.3 us (24%)
  between operations  0.7 us (1%)
    all_gather x4, blocking collectives, swap(): lax.all_gather(values[1], (axis, spare), axis_index_groups=groups)  19.4 us
    all_gather x5, blocking collectives, swap(): lax.all_gather(values[0], axis, axis_index_groups=[[i, i + 1] for i in ra...  17.9 us
    pallas_call x6, Pallas kernels, call(): pl.pallas_call(functools.partial(body, counts), out_shape=outs, in_specs=...  12.3 us

profile of v3, /device:TPU:1, one launch (start us, length us, event | category | flops | bytes accessed | tf_op | source)
XLA Modules:
  0.0 50.3 jit_solution(14999445385395285735)
XLA Ops:
  0.6 0.0 copy-start.2
  0.6 0.0 copy-start
  0.7 0.0 copy-start.1
  0.7 1.5 %rows_out.1 = (f32[4,128,128]{2,1,0:T(8,128)S(1)}, f32[4,128,128]{2,1,0:T(8,128)S(1)}, f32[104,128]{1,0:T(8,128)S(1)}, f32[104,128]{1,0:T(8,128)S(1)}) custom-call(f32[3,4,128,128]{3,2,1,0:T(8,128)} %dm.1, f32[3,4,128,128]{3,2,1,0:T(8,128)} %ds.1, f32[3,4,128,128]{3,2,1,0:T(8,128)} %ct.1, f32[4,128,128]{2,1,0:T(8,128)} %refs_3_.1, f32[4,128,128]{2,1,0:T(8,128)} %refs_4_.1), custom_call_target="tpu_custom_call" | custom-call | tf_op jit(solution)/shard_map/rows_out/pallas_call | solution.py:612
  2.1 4.3 %all-gather = f32[208,128]{1,0:T(8,128)S(1)} all-gather(f32[104,128]{1,0:T(8,128)S(1)} %get-tuple-element.35), channel_id=2, replica_groups={{0,8},{16,24},{1,9},{17,25},{2,10},{18,26},{3,11},{19,27},{4,12},{20,28..., dimensions={0}, use_global_device_ids=true | all-gather | bytes 159744 | tf_op jit(solution)/shard_map/all_gather | solution.py:40
  6.4 3.6 %all-gather.1 = f32[208,128]{1,0:T(8,128)S(1)} all-gather(f32[104,128]{1,0:T(8,128)S(1)} %get-tuple-element.36), channel_id=3, replica_groups={{8,16},{12,20},{0,4},{24,28},{9,17},{13,21},{1,5},{25,29},{10,18},{14,2..., dimensions={0}, use_global_device_ids=true | all-gather | bytes 159744 | tf_op jit(solution)/shard_map/all_gather | solution.py:45
  10.1 0.0 copy-done.2
  10.1 0.0 copy-done
  10.1 0.0 copy-done.1
  10.1 3.5 %build.1 = (f32[11,4,160,128]{3,2,1,0:T(8,128)S(1)}, f32[11,160,128]{2,1,0:T(8,128)S(1)}, f32[144,128]{1,0:T(8,128)S(1)}) custom-call(f32[3,4,128,128]{3,2,1,0:T(8,128)S(1)} %copy-done, f32[3,4,128,128]{3,2,1,0:T(8,128)S(1)} %copy-done.1, f32[3,4,128,128]{3,2,1,0:T(8,128)S(1)} %copy-done.2, f32[4,128,128]{2,1,0:T(8,128)S(1)} %get-tuple-element.33.w, ...), custom_call_target="tpu_custom_call" | custom-call | tf_op jit(solution)/shard_map/build/pallas_call | solution.py:612
  13.5 3.9 %all-gather.2 = f32[288,128]{1,0:T(8,128)S(1)} all-gather(f32[144,128]{1,0:T(8,128)S(1)} %get-tuple-element.39), channel_id=4, replica_groups={{0,4},{1,5},{2,6},{3,7},{8,12},{9,13},{10,14},{11,15},{16,20},{17,21},{..., dimensions={0}, use_global_device_ids=true | all-gather | bytes 221184 | tf_op jit(solution)/shard_map/all_gather | solution.py:40
  17.4 2.0 %strips_and_values.1 = (f32[11,160,128]{2,1,0:T(8,128)S(1)}, f32[2,4,160,128]{3,2,1,0:T(8,128)S(1)}, f32[2,160,128]{2,1,0:T(8,128)S(1)}, f32[336,128]{1,0:T(8,128)S(1)}, f32[336,128]{1,0:T(8,128)S(1)}) custom-call(f32[11,4,160,128]{3,2,1,0:T(8,128)S(1)} %get-tuple-element.37.em, f32[11,160,128]{2,1,0:T(8,128)S(1)} %get-tuple-element.38.es, ...), custom_call_target="tpu_custom_call" | custom-call | tf_op jit(solution)/shard_map/strips_and_values/pallas_call | solution.py:612
  19.4 5.5 %all-gather.3 = f32[672,128]{1,0:T(8,128)S(1)} all-gather(f32[336,128]{1,0:T(8,128)S(1)} %get-tuple-element.43), channel_id=5, replica_groups={{0,1},{2,3},{4,5},{6,7},{8,9},{10,11},{12,13},{14,15},{16,17},{18,19},{..., dimensions={0}, use_global_device_ids=true | all-gather | bytes 516096 | tf_op jit(solution)/shard_map/all_gather | solution.py:40
  24.9 6.0 %all-gather.4 = f32[672,128]{1,0:T(8,128)S(1)} all-gather(f32[336,128]{1,0:T(8,128)S(1)} %get-tuple-element.44), channel_id=6, replica_groups={{1,2},{5,6},{0,4},{3,7},{9,10},{13,14},{8,12},{11,15},{17,18},{21,22},{..., dimensions={0}, use_global_device_ids=true | all-gather | bytes 516096 | tf_op jit(solution)/shard_map/all_gather | solution.py:45
  30.9 1.6 %first_step.1 = (f32[4,160,128]{2,1,0:T(8,128)S(1)}, f32[160,128]{1,0:T(8,128)S(1)}, f32[4,160,128]{2,1,0:T(8,128)S(1)}, f32[160,128]{1,0:T(8,128)S(1)}, f32[4,1...) custom-call(f32[11,4,160,128]{3,2,1,0:T(8,128)S(1)} %get-tuple-eleme, ...), custom_call_target="tpu_custom_call" | custom-call | tf_op jit(solution)/shard_map/first_step/pallas_call | solution.py:612
  32.6 2.0 %all-gather.5 = f32[336,128]{1,0:T(8,128)S(1)} all-gather(f32[168,128]{1,0:T(8,128)S(1)} %get-tuple-element.52), channel_id=7, replica_groups={{0,1},{2,3},{4,5},{6,7},{8,9},{10,11},{12,13},{14,15},{16,17},{18,19},{..., dimensions={0}, use_global_device_ids=true | all-gather | bytes 258048 | tf_op jit(solution)/shard_map/all_gather | solution.py:40
  34.6 4.9 %all-gather.6 = f32[336,128]{1,0:T(8,128)S(1)} all-gather(f32[168,128]{1,0:T(8,128)S(1)} %get-tuple-element.53), channel_id=8, replica_groups={{1,2},{5,6},{0,4},{3,7},{9,10},{13,14},{8,12},{11,15},{17,18},{21,22},{..., dimensions={0}, use_global_device_ids=true | all-gather | bytes 258048 | tf_op jit(solution)/shard_map/all_gather | solution.py:45
  39.5 1.9 %second_step.1 = (f32[3,4,160,128]{3,2,1,0:T(8,128)S(1)}, f32[4,160,128]{2,1,0:T(8,128)S(1)}, f32[160,128]{1,0:T(8,128)S(1)}, f32[160,128]{1,0:T(8,128)S(1)}, f3...) custom-call(f32[11,4,160,128]{3,2,1,0:T(8,128)S(1)} %get-tuple-eleme, ...), custom_call_target="tpu_custom_call" | custom-call | tf_op jit(solution)/shard_map/second_step/pallas_call | solution.py:612
  41.3 2.2 %all-gather.7 = f32[336,128]{1,0:T(8,128)S(1)} all-gather(f32[168,128]{1,0:T(8,128)S(1)} %get-tuple-element.61), channel_id=9, replica_groups={{0,1},{2,3},{4,5},{6,7},{8,9},{10,11},{12,13},{14,15},{16,17},{18,19},{..., dimensions={0}, use_global_device_ids=true | all-gather | bytes 258048 | tf_op jit(solution)/shard_map/all_gather | solution.py:40
  43.5 4.9 %all-gather.8 = f32[336,128]{1,0:T(8,128)S(1)} all-gather(f32[168,128]{1,0:T(8,128)S(1)} %get-tuple-element.62), channel_id=10, replica_groups={{1,2},{5,6},{0,4},{3,7},{9,10},{13,14},{8,12},{11,15},{17,18},{21,22},{..., dimensions={0}, use_global_device_ids=true | all-gather | bytes 258048 | tf_op jit(solution)/shard_map/all_gather | solution.py:45
  48.4 1.8 %finish.1 = (f32[3,4,128,128]{3,2,1,0:T(8,128)}, f32[4,128,128]{2,1,0:T(8,128)}, f32[4,128,128]{2,1,0:T(8,128)}) custom-call(f32[3,4,160,128]{3,2,1,0:T(8,128)S(1)} %get-tuple-element.54.x, f32[4,160,128]{2,1,0:T(8,128)S(1)} %get-tuple-element.55.r2, f32[160,128]{1,0:T(8,128)S(1)} %get-tuple-element.56.r2s, f32[160,128]{1,0:T(8,128)S(1)} %get-tuple-element.57.top, ...), custom_call_target="tpu_custom_call" | custom-call | tf_op jit(solution)/shard_map/finish/pallas_call | solution.py:612
Async XLA Ops:
  0.6 9.4 %copy-start.2 = (f32[3,4,128,128]{3,2,1,0:T(8,128)S(1)}, f32[3,4,128,128]{3,2,1,0:T(8,128)}, u32[]{:S(2)}) copy-start(f32[3,4,128,128]{3,2,1,0:T(8,128)} %ct.1) | copy-start | bytes 2359300
  0.6 9.4 %copy-start = (f32[3,4,128,128]{3,2,1,0:T(8,128)S(1)}, f32[3,4,128,128]{3,2,1,0:T(8,128)}, u32[]{:S(2)}) copy-start(f32[3,4,128,128]{3,2,1,0:T(8,128)} %dm.1) | copy-start | bytes 2359300
  0.7 9.4 %copy-start.1 = (f32[3,4,128,128]{3,2,1,0:T(8,128)S(1)}, f32[3,4,128,128]{3,2,1,0:T(8,128)}, u32[]{:S(2)}) copy-start(f32[3,4,128,128]{3,2,1,0:T(8,128)} %ds.1) | copy-start | bytes 2359300

commit v4 on v3

--- a/solution.py
+++ b/solution.py
@@ -17,8 +17,10 @@
 WEIGHT, DATA = 9, 10
 PAD = 16
 SUB = 8
-UNROLL = 3
-TOGETHER = 3
+UNROLL = 18
+TOGETHER = 6
+PAIRED = 4
+LAST = 16
 LANES = 128
 GROUP = 16
 
@@ -83,6 +85,22 @@
 
 
 ALL = slice(None)
+
+
+def in_groups(count, together, step):
+    while count % together:
+        together -= 1
+
+    def body(t):
+        later = Later()
+        for u in range(together):
+            step(t * together + u, later)
+        later.flush()
+
+    if together == count:
+        body(0)
+    else:
+        pl.loop(0, count // together)(body)
 
 
 def batches(count, size):
@@ -223,24 +241,24 @@
     packing = [pack_lanes(lane, planes, link.even if p == 0 else link.odd) for p in range(ny)]
 
     def tile(row, read, later):
-        packed = [None] * ny
         for f in range(FIELDS):
             strip = jnp.full((SUB, LANES), 1.0 if f == WEIGHT else 0.0, jnp.float32)
             for k in range(planes):
                 strip = jnp.where(jnp.logical_and(own, plane_of == k + 1), take(read(f, k), edges), strip)
             later.put(es, (f, pl.ds(row, SUB), ALL), strip)
-            for p in range(ny):
-                moved = take(strip, packing[p])
-                packed[p] = moved if f == 0 else jnp.where(lane >= column_lanes(planes)[f], moved, packed[p])
+
+    def pack(t, later):
+        row = pl.multiple_of(t * SUB, SUB)
         for p in range(ny):
-            later.put(outs[p], (pl.ds(row - SUB, SUB), ALL), packed[p])
-
-    @pl.loop(0, rows // SUB)
-    def _(t):
+            out = take(es[0, pl.ds(row + SUB, SUB), :], packing[p])
+            for f in range(1, FIELDS):
+                moved = take(es[f, pl.ds(row + SUB, SUB), :], packing[p])
+                out = jnp.where(lane >= column_lanes(planes)[f], moved, out)
+            later.put(outs[p], (pl.ds(row, SUB), ALL), out)
+
+    def inner(t, later):
         inside = pl.multiple_of(t * SUB, SUB)
         row = pl.multiple_of(t * SUB + PAD, SUB)
-
-        later = Later()
 
         def read(f, k):
             x = src_rows(src[f], k, pl.ds(inside, SUB))
@@ -249,14 +267,14 @@
             return x
 
         tile(row, read, later)
-        later.flush()
-
-    @pl.loop(0, 2)
-    def _(t):
-        later = Later()
-        row = pl.multiple_of(PAD - SUB + t * (rows + SUB), SUB)
-        tile(row, lambda f, k: em[f, k, pl.ds(row, SUB), :], later)
-        later.flush()
+
+    def halos(t, later):
+        for row in (PAD - SUB, PAD + rows):
+            tile(row, lambda f, k: em[f, k, pl.ds(row, SUB), :], later)
+
+    in_groups(rows // SUB, PAIRED, inner)
+    in_groups(1, 1, halos)
+    in_groups(sizes(rows)[0], UNROLL, pack)
 
 
 def fold(strip, group, out, base, tiles):
@@ -377,15 +395,8 @@
                 x = x - INVERSE * em[DATA, k, at, :]
                 later.put(v, (m, k, at, ALL), jnp.where(keep, x, 0.0))
 
-    for body in (strips, values):
-
-        @pl.loop(0, tiles // UNROLL)
-        def _(t):
-            later = Later()
-            for u in range(UNROLL):
-                body(t * UNROLL + u, later)
-            later.flush()
-
+    in_groups(tiles, UNROLL, strips)
+    in_groups(tiles, UNROLL, values)
     plane_out(
         Link("gz", counts["gz"]),
         outs,
@@ -475,14 +486,18 @@
 
 
 def over_tiles(tiles, planes, step):
+    together = TOGETHER
+    while tiles % together:
+        together -= 1
+
     def body(t, carried):
         later = Later()
-        for u in range(TOGETHER):
-            carried = step(t * TOGETHER + u, carried, later)
+        for u in range(together):
+            carried = step(t * together + u, carried, later)
         later.flush()
         return tuple(carried)
 
-    lax.fori_loop(0, tiles // TOGETHER, body, (jnp.zeros((SUB, LANES), jnp.float32),) * (planes + 1))
+    lax.fori_loop(0, tiles // together, body, (jnp.zeros((SUB, LANES), jnp.float32),) * (planes + 1))
 
 
 def chooser(mid, first, ghost, planes):
@@ -592,19 +607,18 @@
     below, above = plane_in(link, got)
     settle(r2.at[0], r2s, top, tops, below, above, 0, link.after, first, ghost, strip, planes, rows)
 
-    @pl.loop(0, rows // SUB, unroll=2)
-    def _(t):
+    def step(t, later):
         row = pl.multiple_of(SUB * t + PAD, SUB)
         at, to = pl.ds(row, SUB), pl.ds(pl.multiple_of(SUB * t, SUB), SUB)
         spread = Around(chooser(r2, first, ghost, planes), strip, planes, row, lane)
-        later = Later()
         for k in range(planes):
             down = spread.steps(k)
             for a in range(3):
                 later.put(grad, (a, k, to, ALL), x[a, k, at, :] + down[a])
             later.put(weight_grad, (k, to, ALL), wg[k, at, :])
             later.put(data_grad, (k, to, ALL), INVERSE * (dg[k, at, :] + spread.now[k]))
-        later.flush()
+
+    in_groups(rows // SUB, LAST, step)
 
 
 def call(body, counts, operands, outs, scratch=(), space=pltpu.VMEM, grant=16):

time: 51.1 us -> 47.1 us (0.922)
  Pallas kernels: 12.3 us -> 8.23 us
    pallas_call x6, Pallas kernels: 12.3 us -> 8.23 us  [call(): pl.pallas_call(functools.partial(body, counts), out_shape=outs, in_specs=...]
where the time goes in v4:
time: 47.1 us; the launch traced here: 46.2 us
  blocking collectives  37.3 us (79%)
  Pallas kernels  8.23 us (17%)
  between operations  0.7 us (1%)
    all_gather x4, blocking collectives, swap(): lax.all_gather(values[1], (axis, spare), axis_index_groups=groups)  19.4 us
    all_gather x5, blocking collectives, swap(): lax.all_gather(values[0], axis, axis_index_groups=[[i, i + 1] for i in ra...  17.9 us
    pallas_call x6, Pallas kernels, call(): pl.pallas_call(functools.partial(body, counts), out_shape=outs, in_specs=...  8.23 us

profile of v4, /device:TPU:1, one launch (start us, length us, event | category | flops | bytes accessed | tf_op | source)
XLA Modules:
  0.0 46.2 jit_solution(15296034919355893)
XLA Ops:
  0.6 0.0 copy-start.2
  0.6 0.0 copy-start
  0.7 0.0 copy-start.1
  0.7 1.5 %rows_out.1 = (f32[4,128,128]{2,1,0:T(8,128)S(1)}, f32[4,128,128]{2,1,0:T(8,128)S(1)}, f32[104,128]{1,0:T(8,128)S(1)}, f32[104,128]{1,0:T(8,128)S(1)}) custom-call(f32[3,4,128,128]{3,2,1,0:T(8,128)} %dm.1, f32[3,4,128,128]{3,2,1,0:T(8,128)} %ds.1, f32[3,4,128,128]{3,2,1,0:T(8,128)} %ct.1, f32[4,128,128]{2,1,0:T(8,128)} %refs_3_.1, f32[4,128,128]{2,1,0:T(8,128)} %refs_4_.1), custom_call_target="tpu_custom_call" | custom-call | tf_op jit(solution)/shard_map/rows_out/pallas_call | solution.py:626
  2.1 4.3 %all-gather = f32[208,128]{1,0:T(8,128)S(1)} all-gather(f32[104,128]{1,0:T(8,128)S(1)} %get-tuple-element.35), channel_id=2, replica_groups={{0,8},{16,24},{1,9},{17,25},{2,10},{18,26},{3,11},{19,27},{4,12},{20,28..., dimensions={0}, use_global_device_ids=true | all-gather | bytes 159744 | tf_op jit(solution)/shard_map/all_gather | solution.py:42
  6.4 3.6 %all-gather.1 = f32[208,128]{1,0:T(8,128)S(1)} all-gather(f32[104,128]{1,0:T(8,128)S(1)} %get-tuple-element.36), channel_id=3, replica_groups={{8,16},{12,20},{0,4},{24,28},{9,17},{13,21},{1,5},{25,29},{10,18},{14,2..., dimensions={0}, use_global_device_ids=true | all-gather | bytes 159744 | tf_op jit(solution)/shard_map/all_gather | solution.py:47
  10.1 0.0 copy-done.2
  10.1 0.0 copy-done
  10.1 0.0 copy-done.1
  10.1 1.5 %build.1 = (f32[11,4,160,128]{3,2,1,0:T(8,128)S(1)}, f32[11,160,128]{2,1,0:T(8,128)S(1)}, f32[144,128]{1,0:T(8,128)S(1)}) custom-call(f32[3,4,128,128]{3,2,1,0:T(8,128)S(1)} %copy-done, f32[3,4,128,128]{3,2,1,0:T(8,128)S(1)} %copy-done.1, f32[3,4,128,128]{3,2,1,0:T(8,128)S(1)} %copy-done.2, f32[4,128,128]{2,1,0:T(8,128)S(1)} %get-tuple-element.33.w, ...), custom_call_target="tpu_custom_call" | custom-call | tf_op jit(solution)/shard_map/build/pallas_call | solution.py:626
  11.6 3.9 %all-gather.2 = f32[288,128]{1,0:T(8,128)S(1)} all-gather(f32[144,128]{1,0:T(8,128)S(1)} %get-tuple-element.39), channel_id=4, replica_groups={{0,4},{1,5},{2,6},{3,7},{8,12},{9,13},{10,14},{11,15},{16,20},{17,21},{..., dimensions={0}, use_global_device_ids=true | all-gather | bytes 221184 | tf_op jit(solution)/shard_map/all_gather | solution.py:42
  15.4 1.2 %strips_and_values.1 = (f32[11,160,128]{2,1,0:T(8,128)S(1)}, f32[2,4,160,128]{3,2,1,0:T(8,128)S(1)}, f32[2,160,128]{2,1,0:T(8,128)S(1)}, f32[336,128]{1,0:T(8,128)S(1)}, f32[336,128]{1,0:T(8,128)S(1)}) custom-call(f32[11,4,160,128]{3,2,1,0:T(8,128)S(1)} %get-tuple-element.37.em, f32[11,160,128]{2,1,0:T(8,128)S(1)} %get-tuple-element.38.es, ...), custom_call_target="tpu_custom_call" | custom-call | tf_op jit(solution)/shard_map/strips_and_values/pallas_call | solution.py:626
  16.6 5.5 %all-gather.3 = f32[672,128]{1,0:T(8,128)S(1)} all-gather(f32[336,128]{1,0:T(8,128)S(1)} %get-tuple-element.43), channel_id=5, replica_groups={{0,1},{2,3},{4,5},{6,7},{8,9},{10,11},{12,13},{14,15},{16,17},{18,19},{..., dimensions={0}, use_global_device_ids=true | all-gather | bytes 516096 | tf_op jit(solution)/shard_map/all_gather | solution.py:42
  22.1 6.0 %all-gather.4 = f32[672,128]{1,0:T(8,128)S(1)} all-gather(f32[336,128]{1,0:T(8,128)S(1)} %get-tuple-element.44), channel_id=6, replica_groups={{1,2},{5,6},{0,4},{3,7},{9,10},{13,14},{8,12},{11,15},{17,18},{21,22},{..., dimensions={0}, use_global_device_ids=true | all-gather | bytes 516096 | tf_op jit(solution)/shard_map/all_gather | solution.py:47
  28.1 1.2 %first_step.1 = (f32[4,160,128]{2,1,0:T(8,128)S(1)}, f32[160,128]{1,0:T(8,128)S(1)}, f32[4,160,128]{2,1,0:T(8,128)S(1)}, f32[160,128]{1,0:T(8,128)S(1)}, f32[4,1...) custom-call(f32[11,4,160,128]{3,2,1,0:T(8,128)S(1)} %get-tuple-eleme, ...), custom_call_target="tpu_custom_call" | custom-call | tf_op jit(solution)/shard_map/first_step/pallas_call | solution.py:626
  29.4 2.0 %all-gather.5 = f32[336,128]{1,0:T(8,128)S(1)} all-gather(f32[168,128]{1,0:T(8,128)S(1)} %get-tuple-element.52), channel_id=7, replica_groups={{0,1},{2,3},{4,5},{6,7},{8,9},{10,11},{12,13},{14,15},{16,17},{18,19},{..., dimensions={0}, use_global_device_ids=true | all-gather | bytes 258048 | tf_op jit(solution)/shard_map/all_gather | solution.py:42
  31.4 4.9 %all-gather.6 = f32[336,128]{1,0:T(8,128)S(1)} all-gather(f32[168,128]{1,0:T(8,128)S(1)} %get-tuple-element.53), channel_id=8, replica_groups={{1,2},{5,6},{0,4},{3,7},{9,10},{13,14},{8,12},{11,15},{17,18},{21,22},{..., dimensions={0}, use_global_device_ids=true | all-gather | bytes 258048 | tf_op jit(solution)/shard_map/all_gather | solution.py:47
  36.3 1.6 %second_step.1 = (f32[3,4,160,128]{3,2,1,0:T(8,128)S(1)}, f32[4,160,128]{2,1,0:T(8,128)S(1)}, f32[160,128]{1,0:T(8,128)S(1)}, f32[160,128]{1,0:T(8,128)S(1)}, f3...) custom-call(f32[11,4,160,128]{3,2,1,0:T(8,128)S(1)} %get-tuple-eleme, ...), custom_call_target="tpu_custom_call" | custom-call | tf_op jit(solution)/shard_map/second_step/pallas_call | solution.py:626
  37.8 2.2 %all-gather.7 = f32[336,128]{1,0:T(8,128)S(1)} all-gather(f32[168,128]{1,0:T(8,128)S(1)} %get-tuple-element.61), channel_id=9, replica_groups={{0,1},{2,3},{4,5},{6,7},{8,9},{10,11},{12,13},{14,15},{16,17},{18,19},{..., dimensions={0}, use_global_device_ids=true | all-gather | bytes 258048 | tf_op jit(solution)/shard_map/all_gather | solution.py:42
  40.0 4.9 %all-gather.8 = f32[336,128]{1,0:T(8,128)S(1)} all-gather(f32[168,128]{1,0:T(8,128)S(1)} %get-tuple-element.62), channel_id=10, replica_groups={{1,2},{5,6},{0,4},{3,7},{9,10},{13,14},{8,12},{11,15},{17,18},{21,22},{..., dimensions={0}, use_global_device_ids=true | all-gather | bytes 258048 | tf_op jit(solution)/shard_map/all_gather | solution.py:47
  44.9 1.3 %finish.1 = (f32[3,4,128,128]{3,2,1,0:T(8,128)}, f32[4,128,128]{2,1,0:T(8,128)}, f32[4,128,128]{2,1,0:T(8,128)}) custom-call(f32[3,4,160,128]{3,2,1,0:T(8,128)S(1)} %get-tuple-element.54.x, f32[4,160,128]{2,1,0:T(8,128)S(1)} %get-tuple-element.55.r2, f32[160,128]{1,0:T(8,128)S(1)} %get-tuple-element.56.r2s, f32[160,128]{1,0:T(8,128)S(1)} %get-tuple-element.57.top, ...), custom_call_target="tpu_custom_call" | custom-call | tf_op jit(solution)/shard_map/finish/pallas_call | solution.py:626
Async XLA Ops:
  0.6 9.4 %copy-start.2 = (f32[3,4,128,128]{3,2,1,0:T(8,128)S(1)}, f32[3,4,128,128]{3,2,1,0:T(8,128)}, u32[]{:S(2)}) copy-start(f32[3,4,128,128]{3,2,1,0:T(8,128)} %ct.1) | copy-start | bytes 2359300
  0.6 9.4 %copy-start = (f32[3,4,128,128]{3,2,1,0:T(8,128)S(1)}, f32[3,4,128,128]{3,2,1,0:T(8,128)}, u32[]{:S(2)}) copy-start(f32[3,4,128,128]{3,2,1,0:T(8,128)} %dm.1) | copy-start | bytes 2359300
  0.7 9.4 %copy-start.1 = (f32[3,4,128,128]{3,2,1,0:T(8,128)S(1)}, f32[3,4,128,128]{3,2,1,0:T(8,128)}, u32[]{:S(2)}) copy-start(f32[3,4,128,128]{3,2,1,0:T(8,128)} %ds.1) | copy-start | bytes 2359300
